TPU v7x, 256 devices: a whole 4x4x8 slice. The times are simulated.
256 devices in a mesh: seq: 32 (over y, z), mp: 8 (over x, core).
Axes of the slice: x: 4, y: 4, z: 8, core: 2. Of those that a mesh axis runs over, the one named last changes fastest.
Arguments:
- out_grad: bfloat16 [16384, 8192], P('seq', 'mp'), may hold values from -6 to 6
- out_weight: bfloat16 [4096, 8192], P('mp'), may hold values from -0.0625 to 0.0625
- queries: bfloat16 [16384, 4096], P('seq', 'mp'), may hold values from -5 to 5
- keys: bfloat16 [64, 128, 4096], P('seq', None, 'mp'), may hold values from -5 to 5
- values: bfloat16 [64, 128, 4096], P('seq', None, 'mp'), may hold values from -6 to 6
- retrieval: int32 [256, 2], replicated, may hold values from 0 to 63, as said below
- counts: int32 [256], P('seq'), may hold values from 1 to 2
Outputs:
- query_grad: bfloat16 [16384, 4096], P('seq', 'mp')
- key_grad: bfloat16 [64, 128, 4096], P('seq', None, 'mp')
- value_grad: bfloat16 [64, 128, 4096], P('seq', None, 'mp')
Inputs may be any that keep to these rules, and one draw needn't show every extreme that they name: `retrieval`: entry e is held by index e // 2 of seq. The 16 neighbour places of one index's blocks name entries of any one owner at most 1 times, and some owner is named exactly 1 times by the blocks of every index.
All inputs are finite; a program needn't handle non-finite values.
Results may differ from a plain program's by a relative error of at most 0.0091.
Values may be sent and summed in bfloat16 or wider, within the bound.
A program may use at most 128 MiB of HBM per device.

v0:
```python
import math

import jax
import jax.numpy as jnp
from jax import lax
from jax.sharding import PartitionSpec as P

HEAD = 128
BLOCK = 64
NEIGH = 2


def rank_slots(owners):
    slot_total = owners.shape[-1]
    earlier_mask = jnp.arange(slot_total)[None, :] < jnp.arange(slot_total)[:, None]
    same_owner = owners[..., :, None] == owners[..., None, :]
    return jnp.sum(same_owner & earlier_mask, axis=-1)


def on_device(out_grad, out_weight, queries, keys, values, retrieval, counts):
    seq_count = lax.axis_size("seq")
    my_index = lax.axis_index("seq")
    tok_rows, head_cols = queries.shape
    entries_here = keys.shape[0]
    nbr_rows = keys.shape[1]
    heads_here = head_cols // HEAD
    blocks_here = tok_rows // BLOCK
    slot_count = blocks_here * NEIGH
    slot_cap = (slot_count + seq_count - 1) // seq_count
    score_scale = 1.0 / math.sqrt(HEAD)
    grad_out = lax.dot_general(
        lax.all_gather(out_grad, "mp", axis=1, tiled=True),
        out_weight,
        (((1,), (1,)), ((), ())),
        preferred_element_type=jnp.float32,
    ).astype(jnp.bfloat16)
    all_lists = retrieval.reshape(seq_count, slot_count)
    owners = all_lists // entries_here
    all_ranks = rank_slots(owners)
    my_lists = lax.dynamic_index_in_dim(all_lists, my_index, 0, keepdims=False)
    my_owner = my_lists // entries_here
    my_rank = lax.dynamic_index_in_dim(all_ranks, my_index, 0, keepdims=False)
    flat_slot = my_owner * slot_cap + my_rank
    chosen = (owners == my_index)[:, None, :] & (
        all_ranks[:, None, :] == jnp.arange(slot_cap)[None, :, None]
    )
    filled = jnp.any(chosen, axis=2)
    picked = jnp.sum(jnp.where(chosen, all_lists[:, None, :] % entries_here, 0), axis=2)
    all_keys, all_values = (
        lax.all_gather(keys, "seq", axis=0, tiled=True),
        lax.all_gather(values, "seq", axis=0, tiled=True),
    )
    slot_keys = jnp.take(all_keys, my_lists, axis=0)
    slot_values = jnp.take(all_values, my_lists, axis=0)
    query_rows = queries.reshape(blocks_here, BLOCK, heads_here, HEAD)
    grad_rows = grad_out.reshape(blocks_here, BLOCK, heads_here, HEAD)
    key_rows = slot_keys.reshape(blocks_here, NEIGH * nbr_rows, heads_here, HEAD)
    value_rows = slot_values.reshape(blocks_here, NEIGH * nbr_rows, heads_here, HEAD)
    live_keys = jnp.arange(NEIGH * nbr_rows)[None, :] < (counts * nbr_rows)[:, None]
    live_mask = live_keys[:, None, None, :]
    scores = (
        jnp.einsum("cqhe,ckhe->chqk", query_rows, key_rows, preferred_element_type=jnp.float32)
        * score_scale
    )
    row_max = jnp.max(jnp.where(live_mask, scores, -jnp.inf), axis=-1, keepdims=True)
    raised = jnp.where(live_mask, jnp.exp(scores - row_max), 0.0)
    attn_weights = raised / jnp.sum(raised, axis=-1, keepdims=True)
    weights_low = attn_weights.astype(jnp.bfloat16)
    attn_out = jnp.einsum(
        "chqk,ckhe->cqhe", weights_low, value_rows, preferred_element_type=jnp.float32
    )
    row_dot = jnp.sum(grad_rows.astype(jnp.float32) * attn_out, axis=-1)
    grad_weights = jnp.einsum(
        "cqhe,ckhe->chqk", grad_rows, value_rows, preferred_element_type=jnp.float32
    )
    grad_scores = attn_weights * (grad_weights - jnp.transpose(row_dot, (0, 2, 1))[..., None])
    grad_low = grad_scores.astype(jnp.bfloat16)
    query_grad = (
        (
            jnp.einsum("chqk,ckhe->cqhe", grad_low, key_rows, preferred_element_type=jnp.float32)
            * score_scale
        )
        .astype(jnp.bfloat16)
        .reshape(tok_rows, head_cols)
    )
    key_terms = (
        (
            jnp.einsum("chqk,cqhe->ckhe", grad_low, query_rows, preferred_element_type=jnp.float32)
            * score_scale
        )
        .astype(jnp.bfloat16)
        .reshape(slot_count, nbr_rows, head_cols)
    )
    value_terms = (
        jnp.einsum("chqk,cqhe->ckhe", weights_low, grad_rows, preferred_element_type=jnp.float32)
        .astype(jnp.bfloat16)
        .reshape(slot_count, nbr_rows, head_cols)
    )
    key_back = (
        jnp.zeros((seq_count * slot_cap, nbr_rows, head_cols), jnp.bfloat16)
        .at[flat_slot]
        .set(key_terms)
        .reshape(seq_count, slot_cap, nbr_rows, head_cols)
    )
    value_back = (
        jnp.zeros((seq_count * slot_cap, nbr_rows, head_cols), jnp.bfloat16)
        .at[flat_slot]
        .set(value_terms)
        .reshape(seq_count, slot_cap, nbr_rows, head_cols)
    )
    back_keys, back_values = (
        lax.all_to_all(key_back, "seq", split_axis=0, concat_axis=0, tiled=True),
        lax.all_to_all(value_back, "seq", split_axis=0, concat_axis=0, tiled=True),
    )
    summing = (
        ((picked[None, :, :] == jnp.arange(entries_here)[:, None, None]) & filled[None, :, :])
        .astype(jnp.bfloat16)
        .reshape(entries_here, seq_count * slot_cap)
    )
    key_grad = (
        jnp.dot(
            summing,
            back_keys.reshape(seq_count * slot_cap, nbr_rows * head_cols),
            preferred_element_type=jnp.float32,
        )
        .astype(jnp.bfloat16)
        .reshape(entries_here, nbr_rows, head_cols)
    )
    value_grad = (
        jnp.dot(
            summing,
            back_values.reshape(seq_count * slot_cap, nbr_rows * head_cols),
            preferred_element_type=jnp.float32,
        )
        .astype(jnp.bfloat16)
        .reshape(entries_here, nbr_rows, head_cols)
    )
    return (query_grad, key_grad, value_grad)


def solution(mesh):
    return jax.shard_map(
        on_device,
        mesh=mesh,
        in_specs=(
            P("seq", "mp"),
            P("mp", None),
            P("seq", "mp"),
            P("seq", None, "mp"),
            P("seq", None, "mp"),
            P(),
            P("seq"),
        ),
        out_specs=(P("seq", "mp"), P("seq", None, "mp"), P("seq", None, "mp")),
        check_vma=False,
    )
```

profile of v0, /device:TPU:8, one launch (start us, length us, event | category | flops | bytes accessed | tf_op | source)
XLA Modules:
  0.0 510.4 jit_solution(1532240102834940952)
XLA Ops:
  11.0 54.0 %all-gather.6.cloned.1.call-done = bf16[512,8192]{1,0:T(8,128)(2,1)} async-done(((bf16[512,1024]{1,0:T(8,128)(2,1)}), bf16[512,8192]{1,0:T(8,128)(2,1)}) %all-gather.6.cloned.1.call-update) | async-done | bytes 8388624 | tf_op jit(solution)/shard_map/all_gather | solution.py:32
  65.0 10.3 %convolution_convert_fusion.2 = bf16[512,512]{1,0:T(8,128)(2,1)S(1)} fusion(bf16[512,8192]{1,0:T(8,128)(2,1)} %all-gather.6.cloned.1.call-done, bf16[512,8192]{1,0:T(8,128)(2,1)} %param.10), kind=kOutput, calls=%fused_computation.31 | convolution fusion | flops 4295229440 | bytes 17301504 | tf_op jit(solution)/shard_map/dot_general | solution.py:31
  75.4 89.7 %all-gather.4.cloned.1.call-done = bf16[64,128,512]{2,1,0:T(8,128)(2,1)} async-done(((bf16[2,128,512]{2,1,0:T(8,128)(2,1)}), bf16[64,128,512]{2,1,0:T(8,128)(2,1)}) %all-gather.4.cloned.1.call-update) | async-done | bytes 8388624 | tf_op jit(solution)/shard_map/all_gather | solution.py:50
  165.1 4.1 gather_fusion
  169.2 94.1 %all-gather.8.cloned.1.call-done = bf16[64,128,512]{2,1,0:T(8,128)(2,1)} async-done(((bf16[2,128,512]{2,1,0:T(8,128)(2,1)}), bf16[64,128,512]{2,1,0:T(8,128)(2,1)}) %all-gather.8.cloned.1.call-update) | async-done | bytes 8388624 | tf_op jit(solution)/shard_map/all_gather | solution.py:51
  263.3 5.4 %gather_fusion.1 = bf16[16,128,512]{2,1,0:T(8,128)(2,1)} fusion(bf16[64,128,512]{2,1,0:T(8,128)(2,1)} %all-gather.8.cloned.1.call-done, s32[1024]{0:T(1024)S(1)} %pad_clamp_fusion), kind=kCustom, calls=%fused_computation.1.clone | custom fusion | bytes 4194368 | tf_op jit(solution)/shard_map/jit(_take)/gather | solution.py:54
  268.7 4.0 broadcast_select_fusion.1
  272.7 2.5 reshape.443
  275.3 0.8 fusion.5
  276.6 1.7 bitcast_reduce_fusion
  278.3 1.3 copy-done.8
  279.7 0.9 convert_bitcast_fusion
  280.6 2.5 copy.120
  283.0 2.7 reshape.496
  285.8 2.4 broadcast.352.clone
  288.2 5.2 %scatter_fusion.1 = bf16[32,128,512]{2,1,0:T(8,128)(2,1)} fusion(bf16[32,128,512]{2,1,0:T(8,128)(2,1)} %broadcast.352.clone, s32[16]{0:T(128)S(1)} %fusion.53, bf16[16,128,512]{2,1,0:T(8,128)(2,1)S(1)} %reshape.496), kind=kCustom, calls=%fused_computation.3 | custom fusion | bytes 6291520 | tf_op jit(solution)/shard_map/scatter | solution.py:108
  293.5 7.4 %all-to-all-start.1 = ((bf16[32,1,128,512]{3,2,1,0:T(8,128)(2,1)}), bf16[32,1,128,512]{3,2,1,0:T(8,128)(2,1)}, u32[]{:S(2)}, u32[]{:S(2)}) async-start(bf16[32,1,128,512]{3,2,1,0:T(8,128)(2,1)} %bitcast.79), calls=%async_computation.1 | async-start | bytes 8388608 | tf_op jit(solution)/shard_map/all_to_all | solution.py:113
  300.9 2.1 reshape.446
  303.0 3.1 fusion.28
  306.4 1.0 multiply_convert_fusion.1
  308.4 2.9 copy.119
  311.4 2.7 reshape.495
  314.1 2.4 broadcast.352.clone.1
  316.6 5.2 %scatter_fusion = bf16[32,128,512]{2,1,0:T(8,128)(2,1)} fusion(bf16[32,128,512]{2,1,0:T(8,128)(2,1)} %broadcast.352.clone.1, s32[16]{0:T(128)S(1)} %fusion.53, bf16[16,128,512]{2,1,0:T(8,128)(2,1)S(1)} %reshape.495), kind=kCustom, calls=%fused_computation.2 | custom fusion | bytes 6291520 | tf_op jit(solution)/shard_map/scatter | solution.py:102
  321.8 72.6 %all-to-all-done.1 = bf16[32,1,128,512]{3,2,1,0:T(8,128)(2,1)} async-done(((bf16[32,1,128,512]{3,2,1,0:T(8,128)(2,1)}), bf16[32,1,128,512]{3,2,1,0:T(8,128)(2,1)}, u32[]{:S(2)}, u32[]{:S(2)}) %all-to-all-start.1) | async-done | bytes 4194336 | tf_op jit(solution)/shard_map/all_to_all | solution.py:113
  394.4 8.6 %all-to-all-start = ((bf16[32,1,128,512]{3,2,1,0:T(8,128)(2,1)}), bf16[32,1,128,512]{3,2,1,0:T(8,128)(2,1)}, u32[]{:S(2)}, u32[]{:S(2)}) async-start(bf16[32,1,128,512]{3,2,1,0:T(8,128)(2,1)} %bitcast.78), calls=%async_computation | async-start | bytes 8388608 | tf_op jit(solution)/shard_map/all_to_all | solution.py:112
  403.3 1.7 fusion.31
  405.3 0.9 copy.162
  406.2 6.5 %copy.126 = bf16[4,8,128,512]{3,1,2,0:T(8,128)(2,1)} copy(bf16[4,8,128,512]{3,2,1,0:T(8,128)(2,1)} %bitcast.27) | data formatting | bytes 8388608
  412.7 84.2 %all-to-all-done = bf16[32,1,128,512]{3,2,1,0:T(8,128)(2,1)} async-done(((bf16[32,1,128,512]{3,2,1,0:T(8,128)(2,1)}), bf16[32,1,128,512]{3,2,1,0:T(8,128)(2,1)}, u32[]{:S(2)}, u32[]{:S(2)}) %all-to-all-start) | async-done | bytes 4194336 | tf_op jit(solution)/shard_map/all_to_all | solution.py:112
  497.0 4.7 copy.124
  503.0 0.8 copy_bitcast_fusion.1
  (47 shorter events, 7.7 us)
Async XLA Ops:
  7.2 3.2 copy-start.6
  7.2 3.7 copy-start.7
  7.2 57.8 %all-gather.6.cloned.1.call-start = ((), (), s32[]{:S(2)}) async-start(), calls=%async_computation.3 | async-start | bytes 9437184 | tf_op jit(solution)/shard_map/all_gather | solution.py:32
  7.9 157.2 %all-gather.4.cloned.1.call-start = ((), (), s32[]{:S(2)}) async-start(), calls=%async_computation.2 | async-start | bytes 8650752 | tf_op jit(solution)/shard_map/all_gather | solution.py:50
  8.7 254.6 %all-gather.8.cloned.1.call-start = ((), (), s32[]{:S(2)}) async-start(), calls=%async_computation.4 | async-start | bytes 8650752 | tf_op jit(solution)/shard_map/all_gather | solution.py:51
  275.3 1.4 copy-start.1
  278.3 1.3 copy-start.8
  293.5 7.4 %copy-start.3 = (bf16[16,128,512]{2,1,0:T(8,128)(2,1)S(1)}, bf16[16,128,512]{2,1,0:T(8,128)(2,1)}, u32[]{:S(2)}) copy-start(bf16[16,128,512]{2,1,0:T(8,128)(2,1)} %get-tuple-element.9) | copy-start | bytes 6291460
  293.5 100.9 %all-to-all-start.1 = ((bf16[32,1,128,512]{3,2,1,0:T(8,128)(2,1)}), bf16[32,1,128,512]{3,2,1,0:T(8,128)(2,1)}, u32[]{:S(2)}, u32[]{:S(2)}) async-start(bf16[32,1,128,512]{3,2,1,0:T(8,128)(2,1)} %bitcast.79), calls=%async_computation.1 | async-start | bytes 8388608 | tf_op jit(solution)/shard_map/all_to_all | solution.py:113
  303.0 3.1 copy-start.4
  303.0 3.5 copy-start.9
  307.5 1.0 copy-start.5
  394.4 8.9 %copy-start.2 = (bf16[8,256,4,128]{3,2,1,0:T(4,128)(2,1)S(1)}, bf16[8,256,4,128]{3,2,1,0:T(4,128)(2,1)}, u32[]{:S(2)}) copy-start(bf16[8,256,4,128]{3,2,1,0:T(4,128)(2,1)} %copy-done.1) | copy-start | bytes 6291460
  394.4 102.6 %all-to-all-start = ((bf16[32,1,128,512]{3,2,1,0:T(8,128)(2,1)}), bf16[32,1,128,512]{3,2,1,0:T(8,128)(2,1)}, u32[]{:S(2)}, u32[]{:S(2)}) async-start(bf16[32,1,128,512]{3,2,1,0:T(8,128)(2,1)} %bitcast.78), calls=%async_computation | async-start | bytes 8388608 | tf_op jit(solution)/shard_map/all_to_all | solution.py:112
  497.0 4.7 copy-start
Sparse Core Ops, SparseCore 0:
  9.9 55.1 all-gather.5
  67.6 97.4 all-gather.3
  167.7 95.5 all-gather.7
where the time goes:
time: 514 us; the launch traced here: 510 us
  waiting for transfers between devices  397 us (77%)
  local copies, waits for them, and re-layouts  57.5 us (11%)
  matrix products  20 us (4%)
  starting transfers between devices  16.1 us (3%)
  between operations  14 us (3%)
  other arithmetic  5.99 us (1%)
    all_gather x1, waiting for transfers between devices, on_device(): lax.all_gather(values, 'seq', axis=0, tiled=True)  94.1 us
    all_gather x1, waiting for transfers between devices, on_device(): lax.all_gather(keys, 'seq', axis=0, tiled=True)  89.7 us
    all_to_all x1, waiting for transfers between devices, on_device(): lax.all_to_all(key_back, 'seq', split_axis=0, concat_axis=0, tiled=True)  84.2 us
    all_to_all x1, waiting for transfers between devices, on_device(): lax.all_to_all(value_back, 'seq', split_axis=0, concat_axis=0, tiled=True)  72.6 us
    all_gather x1, waiting for transfers between devices, on_device(): lax.all_gather(out_grad, 'mp', axis=1, tiled=True)  54 us
    unnamed x24, local copies, waits for them, and re-layouts  15.3 us
    dot_general x1, matrix products, on_device(): lax.dot_general(lax.all_gather(out_grad, 'mp', axis=1, tiled=True), out_w...  10.3 us
  transfers between devices with their start and end apart: 5, of which 5 were waited for; matrix products, arithmetic and copies ran while one was open for 9% of the time, Pallas kernels for 0%

commit v1 on v0

v1 whole, which is shorter than its diff:
```python
import functools
import math

import jax
import jax.numpy as jnp
from jax import lax
from jax.experimental import pallas as pl
from jax.experimental.pallas import tpu as pltpu
from jax.sharding import PartitionSpec as P

HEAD = 128
BLOCK = 64
NEIGH = 2
NX, NY, NZ = 4, 4, 8
OWN = NZ
RDR = NY
LOW = -1e30
MESH = pl.DeviceIdType.MESH
F32, BF16 = jnp.float32, jnp.bfloat16
NT = (((1,), (1,)), ((), ()))
NN = (((1,), (0,)), ((), ()))
TN = (((0,), (0,)), ((), ()))


class Ids:
    def __init__(self):
        self.at = {}

    def __call__(self, *name):
        return self.at.setdefault(name, len(self.at))


MAX_COPIES = 112


def body(
    heads,
    scal,
    vec,
    cnt_in,
    og_in,
    w_in,
    q_in,
    k_in,
    v_in,
    dq_out,
    dk_out,
    dv_out,
    og,
    w,
    acc,
    kv,
    q_all,
    do_all,
    cnt_all,
    q_own,
    do_own,
    ex,
    gw,
    st1,
    st2,
    fac,
    dqp,
    dkv,
    rsr,
    rsl,
    dqb,
    dq_r,
    dq_l,
    ssem,
    rsem,
    lsem,
):
    ids = Ids()
    scale = 1.0 / math.sqrt(HEAD)
    seq, mp = lax.axis_index("seq"), lax.axis_index("mp")
    y, z = seq // NZ, seq % NZ
    x, core = mp // 2, mp % 2
    half = BLOCK * 4

    def at_x(d):
        return (seq, ((x + d) % NX) * 2 + core)

    sibling = (seq, x * 2 + (1 - core))

    def at_y(d):
        return (((y + d) % NY) * NZ + z, mp)

    def at_z(d):
        return (y * NZ + (z + d) % NZ, mp)

    def zz(d):
        return (z + d) % NZ

    started = []

    def send(name, src, dst, dev):
        i = ids(*name)
        cp = pltpu.make_async_remote_copy(
            src_ref=src, dst_ref=dst, send_sem=ssem.at[i], recv_sem=rsem.at[i], device_id=dev, device_id_type=MESH
        )
        cp.start()
        started.append(cp)

    def recv(name, dst):
        i = ids(*name)
        pltpu.make_async_remote_copy(
            src_ref=dst, dst_ref=dst, send_sem=ssem.at[i], recv_sem=rsem.at[i], device_id=sibling, device_id_type=MESH
        ).wait_recv()

    barrier = pltpu.get_barrier_semaphore()
    peers = [at_x(1), at_x(-1), sibling, at_y(1), at_y(-1), at_y(2), at_z(1), at_z(-1)]
    for dev in peers:
        pl.semaphore_signal(barrier, inc=1, device_id=dev, device_id_type=MESH)

    local = []

    def local_copy(src, dst):
        cp = pltpu.make_async_copy(src, dst, lsem.at[len(local)])
        cp.start()
        local.append(cp)

    local_copy(og_in, og.at[mp])
    for c in range(2 * NX):
        local_copy(w_in.at[:, pl.ds(c * 1024, 1024)], w.at[c])
    local_copy(q_in, q_all.at[pl.ds(y * 8, 8)])
    local_copy(k_in, kv.at[0, z])
    local_copy(v_in, kv.at[1, z])
    local_copy(cnt_in, cnt_all.at[pl.ds(y * 8, 8)])

    pl.semaphore_wait(barrier, len(peers))

    def kv_piece(a, o, e):
        return kv.at[a, o, pl.ds(e * 128, 128)]

    pieces = [(a, e) for a in range(2) for e in range(2)]

    def kv_first():
        for a, e in pieces:
            src = (k_in, v_in)[a].at[pl.ds(e * 128, 128)]
            send(("kvR", 1, a, e), src, kv_piece(a, z, e), at_z(1))
            send(("kvL", 1, a, e), src, kv_piece(a, z, e), at_z(-1))

    def kv_hop(k):
        for a, e in pieces:
            if k < 4 or e == 0:
                o = zz(-k)
                recv(("kvR", k, a, e), kv_piece(a, o, e))
                if k < 3 or (k == 3 and e == 0):
                    send(("kvR", k + 1, a, e), kv_piece(a, o, e), kv_piece(a, o, e), at_z(1))
            if k < 4 or e == 1:
                o = zz(k)
                recv(("kvL", k, a, e), kv_piece(a, o, e))
                if k < 3 or (k == 3 and e == 1):
                    send(("kvL", k + 1, a, e), kv_piece(a, o, e), kv_piece(a, o, e), at_z(-1))

    def y_rows(d, h):
        return pl.ds(((y + d) % NY) * 8 + h * 4, 4)

    def y_first(tag, src, buf, h):
        send((tag, "R", h), src, buf.at[y_rows(0, h)], at_y(1))
        send((tag, "L", h), src, buf.at[y_rows(0, h)], at_y(-1))

    def y_on(tag, buf, h):
        d = -1 if h == 0 else 1
        rows = buf.at[y_rows(d, h)]
        recv((tag, "R" if h == 0 else "L", h), rows)
        send((tag, "F", h), rows, rows, at_y(1 if h == 0 else -1))

    def y_rest(tag, buf, h):
        d = 1 if h == 0 else -1
        recv((tag, "L" if h == 0 else "R", h), buf.at[y_rows(d, h)])
        recv((tag, "F", h), buf.at[y_rows(2, h)])

    def y_direct(tag, src, buf, rows):
        mine = buf.at[pl.ds(y * rows, rows)]
        for d in (1, -1, 2):
            send((tag, d), src if src is not None else mine, mine, at_y(d))

    def y_direct_wait(tag, buf, rows):
        for d in (1, -1, 2):
            recv((tag, d), buf.at[pl.ds(((y - d) % NY) * rows, rows)])

    def og_piece(d, h, other=False):
        c = ((x + d) % NX) * 2 + ((1 - core) if other else core)
        return og.at[c, pl.ds(h * half, half)]

    def x_own(h, way):
        src = og_in.at[pl.ds(h * half, half)]
        send(("og", way, h), src, og_piece(0, h), at_x(1 if way == "R" else -1))

    def x_pass(d, h):
        if d == -1:
            name = ("og", "R", h)
        elif d == 1:
            name = ("og", "L", h)
        else:
            name = ("og", "F", h)
        piece = og_piece(d, h)
        recv(name, piece)
        if (d, h) == (-1, 0):
            send(("og", "F", h), piece, piece, at_x(1))
        if (d, h) == (1, 1):
            send(("og", "F", h), piece, piece, at_x(-1))
        send(("ogc", d, h), piece, piece, sibling)

    def x_sib(d, h):
        recv(("ogc", d, h), og_piece(d, h, True))

    def mm(d, h, other, first=False):
        c = ((x + d) % NX) * 2 + ((1 - core) if other else core)
        t = lax.dot_general(og[c, pl.ds(h * half, half), :], w[c], NT, preferred_element_type=F32)
        if first:
            acc[h] = t
        else:
            acc[h] += t

    def grad_done(h):
        do_all[pl.ds(y * 8 + h * 4, 4)] = acc[h].astype(BF16).reshape(4, BLOCK, heads * HEAD)
        y_first("do", do_all.at[y_rows(0, h)], do_all, h)

    lane_reader = lax.broadcasted_iota(jnp.int32, (8, RDR * BLOCK), 1) // BLOCK

    def gather_blocks(src, dst):
        def one(o, carry):
            for r in range(RDR):
                dst[o, pl.ds(r * BLOCK, BLOCK), :] = src[scal[o * RDR + r]]
            return carry

        lax.fori_loop(0, OWN, one, 0)

    def partner_rows(buf, o, base):
        t = buf[scal[base + o * RDR]]
        for r in range(1, RDR):
            t = jnp.where(lane_reader == r, buf[scal[base + o * RDR + r]], t)
        return t

    def cols(h):
        return pl.ds(h * HEAD, HEAD)

    def score_one(o):
        par = vec[o, 2:3, :]
        for h in range(heads):
            s = lax.dot_general(kv[0, o, :, cols(h)], q_own[o, :, cols(h)], NT, preferred_element_type=F32)
            s = jnp.where(par > 0.5, s[128:], s[:128]) * scale
            m = jnp.max(s, axis=0, keepdims=True)
            e = jnp.exp(s - m)
            ex[o, h] = e
            st1[y * OWN + o, h : h + 1, :] = m
            st1[y * OWN + o, heads + h : heads + h + 1, :] = jnp.sum(e, axis=0, keepdims=True)

    def scores(dist):
        if dist in (0, 4):
            score_one(zz(dist))
        else:

            def one(i, carry):
                score_one(zz(dist * (1 - 2 * i)))
                return carry

            lax.fori_loop(0, 2, one, 0)

    def lives(o):
        exists, place = vec[o, 0:1, :], vec[o, 1:2, :]
        short = 2.0 - partner_rows(cnt_all, o, 0)[0:1, :]
        return exists * (1.0 - place * short) > 0.5, exists * (1.0 - (1.0 - place) * short) > 0.5

    def factors():
        def one(o, carry):
            live, live_p = lives(o)
            own = st1[y * OWN + o]
            oth = partner_rows(st1, o, 32)
            m_o, l_o = own[:heads], own[heads : 2 * heads]
            m_p = jnp.where(live_p, oth[:heads], LOW)
            l_p = jnp.where(live_p, oth[heads : 2 * heads], 0.0)
            m = jnp.maximum(m_o, m_p)
            a = jnp.exp(m_o - m)
            f = jnp.where(live, a / (l_o * a + l_p * jnp.exp(m_p - m)), 0.0)
            par = vec[o, 2:3, :]
            fac[o, 0:heads, :] = f * (1.0 - par)
            fac[o, heads : 2 * heads, :] = f * par
            return carry

        lax.fori_loop(0, OWN, one, 0)

    def both(o, h, t0, t1):
        return jnp.concatenate([t0.astype(BF16), t1.astype(BF16)], axis=0)

    def value_one(o):
        for h in range(heads):
            e = ex[o, h]
            p = both(o, h, e * fac[o, h : h + 1, :], e * fac[o, heads + h : heads + h + 1, :])
            t = lax.dot_general(p, do_own[o, :, cols(h)], NN, preferred_element_type=F32)
            dkv[1, o, :, cols(h)] = t.astype(BF16)

    def dots_one(o):
        par = vec[o, 2:3, :]
        for h in range(heads):
            g = lax.dot_general(kv[1, o, :, cols(h)], do_own[o, :, cols(h)], NT, preferred_element_type=F32)
            g = jnp.where(par > 0.5, g[128:], g[:128])
            gw[o, h] = g
            f = fac[o, h : h + 1, :] + fac[o, heads + h : heads + h + 1, :]
            p = (ex[o, h] * f).astype(BF16).astype(F32)
            st2[y * OWN + o, h : h + 1, :] = jnp.sum(p * g, axis=0, keepdims=True)

    def key_one(o):
        _, live_p = lives(o)
        rd = st2[y * OWN + o][:heads] + jnp.where(live_p, partner_rows(st2, o, 32)[:heads], 0.0)
        for h in range(heads):
            e = ex[o, h]
            t = gw[o, h] - rd[h : h + 1]
            d = both(o, h, e * fac[o, h : h + 1, :] * t, e * fac[o, heads + h : heads + h + 1, :] * t)
            dk = lax.dot_general(d, q_own[o, :, cols(h)], NN, preferred_element_type=F32)
            dkv[0, o, :, cols(h)] = (dk * scale).astype(BF16)
            dq = lax.dot_general(d, kv[0, o, :, cols(h)], TN, preferred_element_type=F32)
            dqp[pl.ds(o * RDR, RDR), :, cols(h)] = (dq * scale).astype(BF16).reshape(RDR, BLOCK, HEAD)

    def per_owner(fn, dist):
        if dist in (0, 4):
            fn(zz(dist))
        else:

            def one(i, carry):
                fn(zz(dist * (1 - 2 * i)))
                return carry

            lax.fori_loop(0, 2, one, 0)

    def rs_buf(way, a, k, e):
        return (rsr if way == "R" else rsl).at[a, k, pl.ds(e * 128, 128)]

    def rs_hop(way, a, k, e):
        far = 0 if way == "R" else 1
        sign = 1 if way == "R" else -1
        o = zz(sign * (4 - k))
        piece = dkv.at[a, o, pl.ds(e * 128, 128)]
        if k > 1 or (k == 1 and e == far):
            rs_take(way, a, k - 1, e, o)
        send(("rs" + way, a, k, e), piece, rs_buf(way, a, k, e), at_z(sign))

    def rs_take(way, a, k, e, o):
        buf = rsr if way == "R" else rsl
        recv(("rs" + way, a, k, e), rs_buf(way, a, k, e))
        rows = pl.ds(e * 128, 128)
        dkv[a, o, rows, :] = (dkv[a, o, rows, :].astype(F32) + buf[a, k, rows, :].astype(F32)).astype(BF16)

    def rs_round(a, k):
        for e in range(2):
            for way, far in (("R", 0), ("L", 1)):
                if k > 0 or e == far:
                    rs_hop(way, a, k, e)

    kv_first()
    y_direct("cnt", cnt_in, cnt_all, 8)
    for h in range(2):
        y_first("q", q_in.at[pl.ds(h * 4, 4)], q_all, h)
    x_own(0, "R")
    x_own(0, "L")
    x_own(1, "L")
    for h in range(2):
        send(("ogc", 0, h), og_in.at[pl.ds(h * half, half)], og_piece(0, h), sibling)

    for h in range(2):
        y_on("q", q_all, h)
    for cp in local:
        cp.wait()
    for h in range(2):
        mm(0, h, False, True)
        x_sib(0, h)
        mm(0, h, True)

    kv_hop(1)
    x_pass(-1, 0)
    x_own(1, "R")
    x_pass(1, 0)
    for h in range(2):
        y_rest("q", q_all, h)
    y_direct_wait("cnt", cnt_all, 8)
    gather_blocks(q_all, q_own)
    for d in (-1, 1):
        mm(d, 0, False)
        x_sib(d, 0)
        mm(d, 0, True)
    scores(0)
    scores(1)

    kv_hop(2)
    x_pass(2, 0)
    mm(2, 0, False)
    x_sib(2, 0)
    mm(2, 0, True)
    grad_done(0)
    x_pass(1, 1)
    mm(1, 1, False)
    x_sib(1, 1)
    mm(1, 1, True)
    scores(2)
    y_on("do", do_all, 0)

    kv_hop(3)
    for d in (-1, 2):
        x_pass(d, 1)
        mm(d, 1, False)
        x_sib(d, 1)
        mm(d, 1, True)
    grad_done(1)
    scores(3)
    kv_hop(4)
    scores(4)
    y_direct("st1", None, st1, OWN)
    y_on("do", do_all, 1)
    y_rest("do", do_all, 0)
    y_direct_wait("st1", st1, OWN)
    factors()
    y_rest("do", do_all, 1)
    gather_blocks(do_all, do_own)

    per_owner(value_one, 4)
    rs_round(1, 0)
    per_owner(value_one, 3)
    rs_hop("R", 1, 1, 1)
    rs_hop("L", 1, 1, 0)
    for d in (2, 1, 0):
        per_owner(value_one, d)
    for d in (4, 3, 2):
        per_owner(dots_one, d)
    rs_hop("R", 1, 1, 0)
    rs_hop("L", 1, 1, 1)
    for d in (1, 0):
        per_owner(dots_one, d)
    y_direct("st2", None, st2, OWN)
    rs_round(1, 2)
    y_direct_wait("st2", st2, OWN)

    per_owner(key_one, 4)
    rs_round(0, 0)
    per_owner(key_one, 3)
    rs_hop("R", 0, 1, 1)
    rs_hop("L", 0, 1, 0)
    per_owner(key_one, 2)
    rs_round(1, 3)
    rs_hop("R", 0, 1, 0)
    rs_hop("L", 0, 1, 1)
    for d in (1, 0):
        per_owner(key_one, d)

    def blocks(r, carry):
        def one(b, carry2):
            j = r * 16 + b * 2
            t = dqp[scal[64 + j]].astype(F32) * scal[128 + j].astype(F32)
            t += dqp[scal[65 + j]].astype(F32) * scal[129 + j].astype(F32)
            dqb[r * 8 + b] = t.astype(BF16)
            return carry2

        return lax.fori_loop(0, 8, one, carry)

    lax.fori_loop(0, RDR, blocks, 0)

    def dq_rows(d, h):
        return dqb.at[y_rows(d, h)]

    send(("dq", "R", "far"), dq_rows(2, 0), dq_r.at[pl.ds(8, 4)], at_y(1))
    send(("dq", "L", "far"), dq_rows(2, 1), dq_l.at[pl.ds(8, 4)], at_y(-1))
    send(("dq", "R", 1), dq_rows(1, 1), dq_r.at[pl.ds(4, 4)], at_y(1))
    send(("dq", "L", 0), dq_rows(-1, 0), dq_l.at[pl.ds(0, 4)], at_y(-1))

    rs_round(0, 2)

    def dq_on(way, h, d, buf):
        recv(("dq", way, "far"), buf.at[pl.ds(8, 4)])
        rows = y_rows(d, h)
        dqb[rows] = (dqb[rows].astype(F32) + buf[pl.ds(8, 4)].astype(F32)).astype(BF16)
        send(("dq", way, h), dqb.at[rows], buf.at[pl.ds(h * 4, 4)], at_y(d))

    dq_on("R", 0, 1, dq_r)
    dq_on("L", 1, -1, dq_l)

    def rs_last(a, out):
        for e in range(2):
            rows = pl.ds(e * 128, 128)
            recv(("rsR", a, 3, e), rs_buf("R", a, 3, e))
            recv(("rsL", a, 3, e), rs_buf("L", a, 3, e))
            t = dkv[a, z, rows, :].astype(F32) + rsr[a, 3, rows, :].astype(F32) + rsl[a, 3, rows, :].astype(F32)
            out[rows, :] = t.astype(BF16)

    rs_last(1, dv_out)
    rs_round(0, 3)
    for h in range(2):
        recv(("dq", "R", h), dq_r.at[pl.ds(h * 4, 4)])
        recv(("dq", "L", h), dq_l.at[pl.ds(h * 4, 4)])
    own = dqb[pl.ds(y * 8, 8)].astype(F32)
    dq_out[...] = (own + dq_r[0:8].astype(F32) + dq_l[0:8].astype(F32)).astype(BF16)
    rs_last(0, dk_out)
    for cp in started:
        cp.wait_send()


def on_device(out_grad, out_weight, queries, keys, values, retrieval, counts):
    seq = lax.axis_index("seq")
    y, z = seq // NZ, seq % NZ
    tok, width = queries.shape
    heads = width // HEAD
    blocks = tok // BLOCK
    slots = blocks * NEIGH
    per_owner = keys.shape[0]
    lists = lax.dynamic_index_in_dim(retrieval.reshape(NY, NZ, slots), z, 1, keepdims=False)
    owner = lists // per_owner
    other = owner.reshape(NY, blocks, NEIGH)[:, :, ::-1].reshape(NY, slots)
    match = (owner[None, :, :] == (y * NZ + jnp.arange(NZ))[:, None, None]).astype(jnp.int32)
    place = jnp.arange(slots)[None, None, :]

    def pick(t):
        return jnp.sum(match * t, axis=2)

    reader = jnp.arange(NY)
    block_at = reader[None, :] * blocks + pick(place // NEIGH)
    mine = (owner // NZ == y).astype(jnp.int32)
    pair_at = jnp.where(mine > 0, owner - y * NZ, 0) * NY + reader[:, None]
    scal = jnp.concatenate(
        [block_at.reshape(-1), pick(other[None]).reshape(-1), pair_at.reshape(-1), mine.reshape(-1)]
    ).astype(jnp.int32)
    meta = jnp.stack([pick(jnp.ones_like(place)), pick(place % NEIGH), pick((lists % per_owner)[None])], axis=1)
    vec = jnp.pad(jnp.repeat(meta.astype(F32), BLOCK, axis=2), ((0, 0), (0, 5), (0, 0)))
    cnt = jnp.broadcast_to(counts.astype(F32)[:, None, None], (blocks, 8, NY * BLOCK))

    lanes = NY * BLOCK
    vm = pltpu.VMEM
    scratch = [
        vm((2 * NX, tok, 1024), BF16),
        vm((2 * NX, width, 1024), BF16),
        vm((2, tok // 2, width), F32),
        vm((2, OWN, 256, width), BF16),
        vm((RDR * blocks, BLOCK, width), BF16),
        vm((RDR * blocks, BLOCK, width), BF16),
        vm((RDR * blocks, 8, lanes), F32),
        vm((OWN, lanes, width), BF16),
        vm((OWN, lanes, width), BF16),
        vm((OWN, heads, 128, lanes), F32),
        vm((OWN, heads, 128, lanes), F32),
        vm((NY * OWN, 8, lanes), F32),
        vm((NY * OWN, 8, lanes), F32),
        vm((OWN, 8, lanes), F32),
        vm((OWN * RDR, BLOCK, width), BF16),
        vm((2, OWN, 256, width), BF16),
        vm((2, 4, 256, width), BF16),
        vm((2, 4, 256, width), BF16),
        vm((RDR * blocks, BLOCK, width), BF16),
        vm((12, BLOCK, width), BF16),
        vm((12, BLOCK, width), BF16),
        pltpu.SemaphoreType.DMA((MAX_COPIES,)),
        pltpu.SemaphoreType.DMA((MAX_COPIES,)),
        pltpu.SemaphoreType.DMA((16,)),
    ]
    hbm = pl.BlockSpec(memory_space=pl.ANY)
    vmem = pl.BlockSpec(memory_space=pltpu.VMEM)
    smem = pl.BlockSpec(memory_space=pltpu.SMEM)
    dq, dk, dv = pl.pallas_call(
        functools.partial(body, heads),
        out_shape=(
            jax.ShapeDtypeStruct((blocks, BLOCK, width), BF16),
            jax.ShapeDtypeStruct((256, width), BF16),
            jax.ShapeDtypeStruct((256, width), BF16),
        ),
        in_specs=[smem, vmem, hbm, hbm, hbm, hbm, hbm, hbm],
        out_specs=(vmem, vmem, vmem),
        scratch_shapes=scratch,
        compiler_params=pltpu.CompilerParams(
            collective_id=0, has_side_effects=True, vmem_limit_bytes=63 * 1024 * 1024
        ),
        name="column_attention_grad",
    )(
        scal,
        vec,
        cnt,
        out_grad,
        out_weight,
        queries.reshape(blocks, BLOCK, width),
        keys.reshape(256, width),
        values.reshape(256, width),
    )
    return dq.reshape(tok, width), dk.reshape(keys.shape), dv.reshape(values.shape)


def solution(mesh):
    return jax.shard_map(
        on_device,
        mesh=mesh,
        in_specs=(
            P("seq", "mp"),
            P("mp", None),
            P("seq", "mp"),
            P("seq", None, "mp"),
            P("seq", None, "mp"),
            P(),
            P("seq"),
        ),
        out_specs=(P("seq", "mp"), P("seq", None, "mp"), P("seq", None, "mp")),
        check_vma=False,
    )
```

time: 514 us -> 131 us (0.25)
  waiting for transfers between devices: 397 us -> 0 us
  Pallas kernels: 0 us -> 118 us
  local copies, waits for them, and re-layouts: 57.5 us -> 9.63 us
  matrix products: 20 us -> 0 us
  starting transfers between devices: 16.1 us -> 0 us
  between operations: 14 us -> 0.73 us
    all_gather x3 -> x0, waiting for transfers between devices: 238 us -> none  [the longest x1 94.1 us: on_device(): lax.all_gather(values, 'seq', axis=0, tiled=True)]
    all_to_all x2 -> x0, waiting for transfers between devices: 157 us -> none  [the longest x1 84.2 us: on_device(): lax.all_to_all(key_back, 'seq', split_axis=0, concat_axis=0, tiled=True)]
    pallas_call x0 -> x1, Pallas kernels: none -> 118 us  [on_device(): pl.pallas_call(functools.partial(body, heads), out_shape=(jax.ShapeDtypeS...]
    dot_general x9 -> x0, matrix products: 20 us -> none  [the longest x1 10.3 us: on_device(): lax.dot_general(lax.all_gather(out_grad, 'mp', axis=1, tiled=True), out_w...]
    reshape x13 -> x4, local copies, waits for them, and re-layouts: 16.9 us -> 0.3 us  [the longest x2 0.12 us: on_device(): jnp.repeat(meta.astype(F32), BLOCK, axis=2)]
    all_to_all x2 -> x0, starting transfers between devices: 16 us -> none  [the longest x1 8.63 us: on_device(): lax.all_to_all(key_back, 'seq', split_axis=0, concat_axis=0, tiled=True)]
    scatter x2 -> x0, local copies, waits for them, and re-layouts: 10.4 us -> none  [the longest x1 5.23 us: on_device(): value_back = jnp.zeros((seq_count * slot_cap, nbr_rows, head_cols), jnp.b...]
    gather x2 -> x0, local copies, waits for them, and re-layouts: 9.47 us -> none  [the longest x1 5.41 us: on_device(): slot_values = jnp.take(all_values, my_lists, axis=0)]
  transfers between devices with their start and end apart: 5 -> 0, of which waited for: 5 -> 0; matrix products, arithmetic and copies ran while one was open for 9% -> 0% of each run, Pallas kernels for 0% -> 0%
where the time goes in v1:
time: 131 us; the launch traced here: 130 us
  Pallas kernels  118 us (90%)
  local copies, waits for them, and re-layouts  9.63 us (7%)
  other arithmetic  1.94 us (1%)
    pallas_call x1, Pallas kernels, on_device(): pl.pallas_call(functools.partial(body, heads), out_shape=(jax.ShapeDtypeS...  118 us
    unnamed x4, local copies, waits for them, and re-layouts  6.01 us

profile of v1, /device:TPU:8, one launch (start us, length us, event | category | flops | bytes accessed | tf_op | source)
XLA Modules:
  0.0 130.4 jit_solution(15891907517855599257)
XLA Ops:
  0.7 0.7 convert_element_type.19
  1.3 0.1 add.90
  1.4 0.7 broadcast_in_dim.7.cnt_in
  2.1 0.8 copy.19
  2.9 0.1 reshape.156
  3.0 0.5 broadcast.224
  3.6 0.7 fusion.8
  4.2 0.1 squeeze.10
  4.4 0.1 copy.21
  4.5 0.1 copy.22
  4.6 0.5 fusion.2
  5.1 0.1 broadcast_add_fusion
  5.2 0.1 copy.20
  5.2 0.1 add.88
  5.3 0.1 copy.23
  5.4 0.1 reshape.157
  5.5 0.6 pad_add_fusion.scal
  6.1 0.1 copy.24
  6.2 0.1 broadcast_in_dim.6
  6.3 0.1 reshape.158
  6.4 0.6 pad.4.vec
  7.1 118.1 %column_attention_grad.1 = (bf16[8,64,512]{2,1,0:T(8,128)(2,1)}, bf16[256,512]{1,0:T(8,128)(2,1)}, bf16[256,512]{1,0:T(8,128)(2,1)}) custom-call(s32[192]{0:T(256)} %pad_add_fusion.scal, f32[8,8,256]{2,1,0:T(8,128)} %pad.4.vec, f32[8,8,256]{2,1,0:T(8,128)} %broadcast_in_dim.7.cnt_in, bf16[512,1024]{1,0:T(8,128)(2,1)} %og_in.1, bf16[512,8192]{1,0:T(8,128)(2,1)} %w_in.1, ...), custom_call_target="tpu_custom_call" | custom-call | tf_op jit(solution)/shard_map/column_attention_grad/pallas_call | solution.py:557
  125.2 1.9 %copy.29 = bf16[512,512]{1,0:T(8,128)(2,1)} copy(bf16[512,512]{1,0:T(8,128)(2,1)} %bitcast.15) | data formatting | bytes 1048576
  127.1 1.7 %copy.30 = bf16[2,128,512]{2,1,0:T(8,128)(2,1)} copy(bf16[2,128,512]{2,1,0:T(8,128)(2,1)} %bitcast.19) | data formatting | bytes 524288
  128.8 1.7 %copy.31 = bf16[2,128,512]{2,1,0:T(8,128)(2,1)} copy(bf16[2,128,512]{2,1,0:T(8,128)(2,1)} %bitcast.18) | data formatting | bytes 524288
  (10 shorter events, 0.1 us)

commit v2 on v1

v2 whole, which is shorter than its diff:
```python
import functools
import math

import jax
import jax.numpy as jnp
from jax import lax
from jax.experimental import pallas as pl
from jax.experimental.pallas import tpu as pltpu
from jax.sharding import PartitionSpec as P

HEAD = 128
BLOCK = 64
NEIGH = 2
NX, NY, NZ = 4, 4, 8
OWN = NZ
RDR = NY
LOW = -1e30
MESH = pl.DeviceIdType.MESH
F32, BF16 = jnp.float32, jnp.bfloat16
NT = (((1,), (1,)), ((), ()))
NN = (((1,), (0,)), ((), ()))
TN = (((0,), (0,)), ((), ()))


class Ids:
    def __init__(self):
        self.at = {}

    def __call__(self, *name):
        return self.at.setdefault(name, len(self.at))


MAX_COPIES = 120
LOCAL_IN = 12
BLK, OTHER, PAIR, MINE, EXISTS, PLACE, PARITY = 0, 32, 64, 128, 192, 224, 256


def body(
    heads,
    ret,
    cnt_in,
    og_in,
    w_in,
    q_in,
    k_in,
    v_in,
    dq_out,
    dkv_out,
    og,
    w,
    acc,
    kv,
    q_all,
    do_all,
    cnt_all,
    q_own,
    do_own,
    ex,
    gw,
    st1,
    st2,
    fac,
    dqp,
    dkv,
    rsr,
    rsl,
    dqb,
    dq_far,
    scal,
    ssem,
    rsem,
    lsem,
):
    ids = Ids()
    scale = 1.0 / math.sqrt(HEAD)
    seq, mp = lax.axis_index("seq"), lax.axis_index("mp")
    y, z = seq // NZ, seq % NZ
    x, core = mp // 2, mp % 2
    part = BLOCK * 2

    def at_x(d):
        return (seq, ((x + d) % NX) * 2 + core)

    sibling = (seq, x * 2 + (1 - core))

    def at_y(d):
        return (((y + d) % NY) * NZ + z, mp)

    def at_z(d):
        return (y * NZ + (z + d) % NZ, mp)

    def zz(d):
        return (z + d) % NZ

    started = []

    def send(name, src, dst, dev):
        i = ids(*name)
        cp = pltpu.make_async_remote_copy(
            src_ref=src, dst_ref=dst, send_sem=ssem.at[i], recv_sem=rsem.at[i], device_id=dev, device_id_type=MESH
        )
        cp.start()
        started.append(cp)

    def recv(name, dst):
        i = ids(*name)
        pltpu.make_async_remote_copy(
            src_ref=dst, dst_ref=dst, send_sem=ssem.at[i], recv_sem=rsem.at[i], device_id=sibling, device_id_type=MESH
        ).wait_recv()

    barrier = pltpu.get_barrier_semaphore()
    peers = [at_x(1), at_x(-1), sibling, at_y(1), at_y(-1), at_y(2), at_z(1), at_z(-1)]
    for dev in peers:
        pl.semaphore_signal(barrier, inc=1, device_id=dev, device_id_type=MESH)

    local = []

    def local_copy(src, dst):
        cp = pltpu.make_async_copy(src, dst, lsem.at[len(local)])
        cp.start()
        local.append(cp)

    local_copy(og_in, og.at[mp])
    for c in range(2 * NX):
        local_copy(w_in.at[:, pl.ds(c * 1024, 1024)], w.at[c])
    local_copy(q_in, q_all.at[pl.ds(y * 8, 8)])
    local_copy(k_in, kv.at[0, z])
    local_copy(v_in, kv.at[1, z])

    def tables(r, carry):
        base = (r * NZ + z) * 8
        named = [ret[j % 2, base + j // 2] for j in range(16)]
        owner = [e >> 1 for e in named]
        code = []
        for j in range(16):
            own = owner[j] - y * OWN
            near = (own >= 0) & (own < OWN)
            scal[PAIR + r * 16 + j] = jnp.where(near, own, 0) * RDR + r
            scal[MINE + r * 16 + j] = jnp.where(near, 1, 0)
            code.append((owner[j ^ 1] << 5) + ((named[j] & 1) << 4) + ((j % 2) << 3) + j // 2 + 1024)
        for o in range(OWN):
            t = 0
            for j in range(16):
                t = t + jnp.where(owner[j] == y * OWN + o, code[j], 0)
            scal[BLK + o * RDR + r] = r * 8 + (t & 7)
            scal[PLACE + o * RDR + r] = (t >> 3) & 1
            scal[PARITY + o * RDR + r] = (t >> 4) & 1
            scal[OTHER + o * RDR + r] = (t >> 5) & 31
            scal[EXISTS + o * RDR + r] = t >> 10
        return carry

    for b in range(8):
        cnt_all[y * 8 + b] = jnp.full((8, RDR * BLOCK), cnt_in[b].astype(F32))

    pl.semaphore_wait(barrier, len(peers))

    def kv_piece(a, o, e):
        return kv.at[a, o, pl.ds(e * 128, 128)]

    pieces = [(a, e) for a in range(2) for e in range(2)]

    def kv_first():
        for a, e in pieces:
            src = (k_in, v_in)[a].at[pl.ds(e * 128, 128)]
            send(("kvR", 1, a, e), src, kv_piece(a, z, e), at_z(1))
            send(("kvL", 1, a, e), src, kv_piece(a, z, e), at_z(-1))

    def kv_hop(k):
        for a, e in pieces:
            if k < 4 or e == 0:
                o = zz(-k)
                recv(("kvR", k, a, e), kv_piece(a, o, e))
                if k < 3 or (k == 3 and e == 0):
                    send(("kvR", k + 1, a, e), kv_piece(a, o, e), kv_piece(a, o, e), at_z(1))
            if k < 4 or e == 1:
                o = zz(k)
                recv(("kvL", k, a, e), kv_piece(a, o, e))
                if k < 3 or (k == 3 and e == 1):
                    send(("kvL", k + 1, a, e), kv_piece(a, o, e), kv_piece(a, o, e), at_z(-1))

    def y_rows(d, h, n=4):
        return pl.ds(((y + d) % NY) * 8 + h * n, n)

    def y_first(tag, src, buf, h, n, way):
        send((tag, way, h), src, buf.at[y_rows(0, h, n)], at_y(1 if way == "R" else -1))

    def y_on(tag, buf, h, n):
        even = h % 2 == 0
        rows = buf.at[y_rows(-1 if even else 1, h, n)]
        recv((tag, "R" if even else "L", h), rows)
        send((tag, "F", h), rows, rows, at_y(1 if even else -1))

    def y_rest(tag, buf, h, n):
        even = h % 2 == 0
        recv((tag, "L" if even else "R", h), buf.at[y_rows(1 if even else -1, h, n)])
        recv((tag, "F", h), buf.at[y_rows(2, h, n)])

    def y_direct(tag, src, buf, rows):
        mine = buf.at[pl.ds(y * rows, rows)]
        for d in (1, -1, 2):
            send((tag, d), src if src is not None else mine, mine, at_y(d))

    def y_direct_wait(tag, buf, rows):
        for d in (1, -1, 2):
            recv((tag, d), buf.at[pl.ds(((y - d) % NY) * rows, rows)])

    def og_piece(d, t, other=False):
        c = ((x + d) % NX) * 2 + ((1 - core) if other else core)
        return og.at[c, pl.ds(t * part, part)]

    def x_own(t, way):
        src = og_in.at[pl.ds(t * part, part)]
        send(("og", way, t), src, og_piece(0, t), at_x(1 if way == "R" else -1))

    def x_pass(d, t):
        piece = og_piece(d, t)
        recv(("og", {-1: "R", 1: "L", 2: "F"}[d], t), piece)
        if d == (-1 if t % 2 == 0 else 1):
            send(("og", "F", t), piece, piece, at_x(-d))
        send(("ogc", d, t), piece, piece, sibling)

    def mm(d, t, n=1):
        rows = pl.ds(t * part, n * part)
        for other in (False, True):
            c = ((x + d) % NX) * 2 + ((1 - core) if other else core)
            if other and d == 0:
                recv(("ogc", 0), og.at[c])
            elif other:
                for i in range(t, t + n):
                    recv(("ogc", d, i), og_piece(d, i, True))
            p = lax.dot_general(og[c, rows, :], w[c], NT, preferred_element_type=F32)
            if d == 0 and not other:
                acc[rows, :] = p
            else:
                acc[rows, :] += p

    def grad_done(t):
        do_all[y_rows(0, t, 2)] = acc[pl.ds(t * part, part), :].astype(BF16).reshape(2, BLOCK, heads * HEAD)
        src = do_all.at[y_rows(0, t, 2)]
        for way in ("R", "L"):
            y_first("do", src, do_all, t, 2, way)

    lane_reader = lax.broadcasted_iota(jnp.int32, (8, RDR * BLOCK), 1) // BLOCK

    def lane_pick(base, o):
        t = jnp.full((8, RDR * BLOCK), scal[base + o * RDR])
        for r in range(1, RDR):
            t = jnp.where(lane_reader == r, scal[base + o * RDR + r], t)
        return t.astype(F32)[0:1]

    def gather_blocks(src, dst, o):
        for r in range(RDR):
            dst[o, pl.ds(r * BLOCK, BLOCK), :] = src[scal[BLK + o * RDR + r]]

    def partner_rows(buf, o, base):
        t = buf[scal[base + o * RDR]]
        for r in range(1, RDR):
            t = jnp.where(lane_reader == r, buf[scal[base + o * RDR + r]], t)
        return t

    def cols(h):
        return pl.ds(h * HEAD, HEAD)

    def score_one(o):
        gather_blocks(q_all, q_own, o)
        par = lane_pick(PARITY, o)
        for h in range(heads):
            s = lax.dot_general(kv[0, o, :, cols(h)], q_own[o, :, cols(h)], NT, preferred_element_type=F32)
            s = jnp.where(par > 0.5, s[128:], s[:128]) * scale
            m = jnp.max(s, axis=0, keepdims=True)
            e = jnp.exp(s - m)
            ex[o, h] = e
            st1[y * OWN + o, h : h + 1, :] = m
            st1[y * OWN + o, heads + h : heads + h + 1, :] = jnp.sum(e, axis=0, keepdims=True)

    def scores(dist):
        if dist in (0, 4):
            score_one(zz(dist))
        else:

            def one(i, carry):
                score_one(zz(dist * (1 - 2 * i)))
                return carry

            lax.fori_loop(0, 2, one, 0)

    def lives(o):
        exists, place = lane_pick(EXISTS, o), lane_pick(PLACE, o)
        short = 2.0 - partner_rows(cnt_all, o, BLK)[0:1, :]
        return exists * (1.0 - place * short) > 0.5, exists * (1.0 - (1.0 - place) * short) > 0.5

    def factors():
        def one(o, carry):
            live, live_p = lives(o)
            own = st1[y * OWN + o]
            oth = partner_rows(st1, o, OTHER)
            m_o, l_o = own[:heads], own[heads : 2 * heads]
            m_p = jnp.where(live_p, oth[:heads], LOW)
            l_p = jnp.where(live_p, oth[heads : 2 * heads], 0.0)
            m = jnp.maximum(m_o, m_p)
            a = jnp.exp(m_o - m)
            f = jnp.where(live, a / (l_o * a + l_p * jnp.exp(m_p - m)), 0.0)
            par = lane_pick(PARITY, o)
            fac[o, 0:heads, :] = f * (1.0 - par)
            fac[o, heads : 2 * heads, :] = f * par
            return carry

        lax.fori_loop(0, OWN, one, 0)

    def both(o, h, t0, t1):
        return jnp.concatenate([t0.astype(BF16), t1.astype(BF16)], axis=0)

    def value_one(o):
        gather_blocks(do_all, do_own, o)
        for h in range(heads):
            e = ex[o, h]
            p = both(o, h, e * fac[o, h : h + 1, :], e * fac[o, heads + h : heads + h + 1, :])
            t = lax.dot_general(p, do_own[o, :, cols(h)], NN, preferred_element_type=F32)
            dkv[1, o, :, cols(h)] = t.astype(BF16)

    def dots_one(o):
        par = lane_pick(PARITY, o)
        for h in range(heads):
            g = lax.dot_general(kv[1, o, :, cols(h)], do_own[o, :, cols(h)], NT, preferred_element_type=F32)
            g = jnp.where(par > 0.5, g[128:], g[:128])
            gw[o, h] = g
            f = fac[o, h : h + 1, :] + fac[o, heads + h : heads + h + 1, :]
            p = (ex[o, h] * f).astype(BF16).astype(F32)
            st2[y * OWN + o, h : h + 1, :] = jnp.sum(p * g, axis=0, keepdims=True)

    def key_one(o):
        _, live_p = lives(o)
        rd = st2[y * OWN + o][:heads] + jnp.where(live_p, partner_rows(st2, o, OTHER)[:heads], 0.0)
        for h in range(heads):
            e = ex[o, h]
            t = gw[o, h] - rd[h : h + 1]
            d = both(o, h, e * fac[o, h : h + 1, :] * t, e * fac[o, heads + h : heads + h + 1, :] * t)
            dk = lax.dot_general(d, q_own[o, :, cols(h)], NN, preferred_element_type=F32)
            dkv[0, o, :, cols(h)] = (dk * scale).astype(BF16)
            dq = lax.dot_general(d, kv[0, o, :, cols(h)], TN, preferred_element_type=F32)
            dqp[pl.ds(o * RDR, RDR), :, cols(h)] = (dq * scale).astype(BF16).reshape(RDR, BLOCK, HEAD)

    def per_owner(fn, dist):
        if dist in (0, 4):
            fn(zz(dist))
        else:

            def one(i, carry):
                fn(zz(dist * (1 - 2 * i)))
                return carry

            lax.fori_loop(0, 2, one, 0)

    def rs_buf(way, a, k, e):
        rows = pl.ds(e * 128, 128)
        if k == 3:
            return dkv_out.at[a, 1 if way == "R" else 2, rows]
        return (rsr if way == "R" else rsl).at[a, k, rows]

    def rs_hop(way, a, k, e):
        far = 0 if way == "R" else 1
        sign = 1 if way == "R" else -1
        o = zz(sign * (4 - k))
        piece = dkv.at[a, o, pl.ds(e * 128, 128)]
        if k > 1 or (k == 1 and e == far):
            rs_take(way, a, k - 1, e, o)
        send(("rs" + way, a, k, e), piece, rs_buf(way, a, k, e), at_z(sign))

    def rs_take(way, a, k, e, o):
        buf = rsr if way == "R" else rsl
        recv(("rs" + way, a, k, e), rs_buf(way, a, k, e))
        rows = pl.ds(e * 128, 128)
        dkv[a, o, rows, :] = (dkv[a, o, rows, :].astype(F32) + buf[a, k, rows, :].astype(F32)).astype(BF16)

    def rs_round(a, k):
        for e in range(2):
            for way, far in (("R", 0), ("L", 1)):
                if k > 0 or e == far:
                    rs_hop(way, a, k, e)

    kv_first()
    for t in range(3):
        x_own(t, "R")
        x_own(t, "L")
    for h in range(2):
        src = q_in.at[pl.ds(h * 4, 4)], q_in.at[pl.ds(4 - h * 4, 4)]
        y_first("q", src[0], q_all, h, 4, "R")
        y_first("q", src[1], q_all, 1 - h, 4, "L")
    send(("ogc", 0), og_in, og.at[mp], sibling)
    y_direct("cnt", None, cnt_all, 8)
    lax.fori_loop(0, RDR, tables, 0)

    for h in range(2):
        y_on("q", q_all, h, 4)
    x_pass(-1, 0)
    x_pass(1, 0)
    x_own(3, "L")
    kv_hop(1)
    x_pass(-1, 1)
    x_pass(1, 1)
    for cp in local:
        cp.wait()
    mm(0, 0, 4)
    for h in range(2):
        y_rest("q", q_all, h, 4)
    y_direct_wait("cnt", cnt_all, 8)
    scores(0)
    x_pass(-1, 2)
    x_own(3, "R")
    x_pass(1, 2)
    scores(1)
    mm(-1, 0, 3)
    mm(1, 0, 3)

    kv_hop(2)
    x_pass(2, 0)
    x_pass(1, 3)
    mm(2, 0)
    grad_done(0)
    mm(1, 3)
    scores(2)

    x_pass(2, 1)
    x_pass(2, 2)
    mm(2, 1, 2)
    grad_done(1)
    grad_done(2)
    y_on("do", do_all, 0, 2)
    kv_hop(3)
    x_pass(-1, 3)
    x_pass(2, 3)
    mm(-1, 3)
    mm(2, 3)
    grad_done(3)
    for t in (1, 2):
        y_on("do", do_all, t, 2)
    scores(3)
    kv_hop(4)
    y_on("do", do_all, 3, 2)
    scores(4)
    y_direct("st1", None, st1, OWN)
    for t in range(3):
        y_rest("do", do_all, t, 2)
    y_direct_wait("st1", st1, OWN)
    factors()
    y_rest("do", do_all, 3, 2)

    per_owner(value_one, 4)
    rs_round(1, 0)
    per_owner(value_one, 3)
    rs_hop("R", 1, 1, 1)
    rs_hop("L", 1, 1, 0)
    for d in (2, 1, 0):
        per_owner(value_one, d)
    for d in (4, 3):
        per_owner(dots_one, d)
    rs_hop("R", 1, 1, 0)
    rs_hop("L", 1, 1, 1)
    for d in (2, 1, 0):
        per_owner(dots_one, d)
    y_direct("st2", None, st2, OWN)
    rs_round(1, 2)
    y_direct_wait("st2", st2, OWN)

    per_owner(key_one, 4)
    rs_round(0, 0)
    per_owner(key_one, 3)
    rs_hop("R", 0, 1, 1)
    rs_hop("L", 0, 1, 0)
    per_owner(key_one, 2)
    rs_round(1, 3)
    rs_hop("R", 0, 1, 0)
    rs_hop("L", 0, 1, 1)
    for d in (1, 0):
        per_owner(key_one, d)
    for a in range(2):
        local_copy(dkv.at[a, z], dkv_out.at[a, 0])

    def blocks(r, carry):
        def one(b, carry2):
            j = r * 16 + b * 2
            t = dqp[scal[PAIR + j]].astype(F32) * scal[MINE + j].astype(F32)
            t += dqp[scal[PAIR + 1 + j]].astype(F32) * scal[MINE + 1 + j].astype(F32)
            dqb[r * 8 + b] = t.astype(BF16)
            return carry2

        return lax.fori_loop(0, 8, one, carry)

    lax.fori_loop(0, RDR, blocks, 0)

    def dq_rows(d, h):
        return dqb.at[y_rows(d, h)]

    def dq_land(way, h):
        return dq_out.at[1 if way == "R" else 2, pl.ds(h * 4, 4)]

    send(("dq", "R", "far"), dq_rows(2, 0), dq_far.at[pl.ds(0, 4)], at_y(1))
    send(("dq", "L", "far"), dq_rows(2, 1), dq_far.at[pl.ds(4, 4)], at_y(-1))
    send(("dq", "R", 1), dq_rows(1, 1), dq_land("R", 1), at_y(1))
    send(("dq", "L", 0), dq_rows(-1, 0), dq_land("L", 0), at_y(-1))
    local_copy(dqb.at[pl.ds(y * 8, 8)], dq_out.at[0])

    rs_round(0, 2)

    def dq_on(way, h, d):
        far = pl.ds(h * 4, 4)
        recv(("dq", way, "far"), dq_far.at[far])
        rows = y_rows(d, h)
        dqb[rows] = (dqb[rows].astype(F32) + dq_far[far].astype(F32)).astype(BF16)
        send(("dq", way, h), dqb.at[rows], dq_land(way, h), at_y(d))

    dq_on("R", 0, 1)
    dq_on("L", 1, -1)

    def rs_last(a):
        for e in range(2):
            for way in ("R", "L"):
                recv(("rs" + way, a, 3, e), rs_buf(way, a, 3, e))

    rs_round(0, 3)
    for cp in local[LOCAL_IN:]:
        cp.wait()
    rs_last(1)
    for h in range(2):
        for way in ("R", "L"):
            recv(("dq", way, h), dq_land(way, h))
    rs_last(0)
    for cp in started:
        cp.wait_send()


def sums(dq_in, dkv_in, dq_out, dk_out, dv_out):
    def three(t):
        return (t[0].astype(F32) + t[1].astype(F32) + t[2].astype(F32)).astype(BF16)

    for b in range(8):
        dq_out[pl.ds(b * BLOCK, BLOCK), :] = three(dq_in[:, b])
    for out, a in ((dk_out, 0), (dv_out, 1)):
        for e in range(2):
            out[e] = three(dkv_in[a, :, pl.ds(e * 128, 128), :])


def on_device(out_grad, out_weight, queries, keys, values, retrieval, counts):
    tok, width = queries.shape
    heads = width // HEAD
    blocks = tok // BLOCK
    lanes = NY * BLOCK
    vm = pltpu.VMEM
    scratch = [
        vm((2 * NX, tok, 1024), BF16),
        vm((2 * NX, width, 1024), BF16),
        vm((tok, width), F32),
        vm((2, OWN, 256, width), BF16),
        vm((RDR * blocks, BLOCK, width), BF16),
        vm((RDR * blocks, BLOCK, width), BF16),
        vm((RDR * blocks, 8, lanes), F32),
        vm((OWN, lanes, width), BF16),
        vm((OWN, lanes, width), BF16),
        vm((OWN, heads, 128, lanes), F32),
        vm((OWN, heads, 128, lanes), F32),
        vm((NY * OWN, 8, lanes), F32),
        vm((NY * OWN, 8, lanes), F32),
        vm((OWN, 8, lanes), F32),
        vm((OWN * RDR, BLOCK, width), BF16),
        vm((2, OWN, 256, width), BF16),
        vm((2, 3, 256, width), BF16),
        vm((2, 3, 256, width), BF16),
        vm((RDR * blocks, BLOCK, width), BF16),
        vm((8, BLOCK, width), BF16),
        pltpu.SMEM((288,), jnp.int32),
        pltpu.SemaphoreType.DMA((MAX_COPIES,)),
        pltpu.SemaphoreType.DMA((MAX_COPIES,)),
        pltpu.SemaphoreType.DMA((16,)),
    ]
    hbm = pl.BlockSpec(memory_space=pl.ANY)
    vmem = pl.BlockSpec(memory_space=pltpu.VMEM)
    smem = pl.BlockSpec(memory_space=pltpu.SMEM)
    dq_parts, dkv_parts = pl.pallas_call(
        functools.partial(body, heads),
        out_shape=(
            jax.ShapeDtypeStruct((3, blocks, BLOCK, width), BF16),
            jax.ShapeDtypeStruct((2, 3, 256, width), BF16),
        ),
        in_specs=[smem, smem, hbm, hbm, hbm, hbm, hbm],
        out_specs=(hbm, hbm),
        scratch_shapes=scratch,
        compiler_params=pltpu.CompilerParams(
            collective_id=0, has_side_effects=True, vmem_limit_bytes=63 * 1024 * 1024
        ),
        name="column_attention_grad",
    )(
        retrieval.T,
        counts,
        out_grad,
        out_weight,
        queries.reshape(blocks, BLOCK, width),
        keys.reshape(256, width),
        values.reshape(256, width),
    )
    return pl.pallas_call(
        sums,
        out_shape=(
            jax.ShapeDtypeStruct(queries.shape, BF16),
            jax.ShapeDtypeStruct(keys.shape, BF16),
            jax.ShapeDtypeStruct(values.shape, BF16),
        ),
        in_specs=[vmem, vmem],
        out_specs=(vmem, vmem, vmem),
        name="sums_of_sides",
    )(dq_parts, dkv_parts)


def solution(mesh):
    return jax.shard_map(
        on_device,
        mesh=mesh,
        in_specs=(
            P("seq", "mp"),
            P("mp", None),
            P("seq", "mp"),
            P("seq", None, "mp"),
            P("seq", None, "mp"),
            P(),
            P("seq"),
        ),
        out_specs=(P("seq", "mp"), P("seq", None, "mp"), P("seq", None, "mp")),
        check_vma=False,
    )
```

time: 131 us -> 115 us (0.88)
  local copies, waits for them, and re-layouts: 9.63 us -> 0 us
  Pallas kernels: 118 us -> 114 us
  other arithmetic: 1.94 us -> 0 us
    pallas_call x1, Pallas kernels: 118 us -> 111 us  [on_device(): pl.pallas_call(functools.partial(body, heads), out_shape=(jax.ShapeDtypeS...]
    unnamed x4 -> x0, local copies, waits for them, and re-layouts: 6.01 us -> none
    pallas_call x0 -> x1, Pallas kernels: none -> 3.04 us  [on_device(): pl.pallas_call(sums, out_shape=(jax.ShapeDtypeStruct(queries.shape, BF16)...]
where the time goes in v2:
time: 115 us
  Pallas kernels  114 us (99%)
    pallas_call x1, Pallas kernels, on_device(): pl.pallas_call(functools.partial(body, heads), out_shape=(jax.ShapeDtypeS...  111 us
    pallas_call x1, Pallas kernels, on_device(): pl.pallas_call(sums, out_shape=(jax.ShapeDtypeStruct(queries.shape, BF16)...  3.04 us

profile of v2, /device:TPU:8, one launch (start us, length us, event | category | flops | bytes accessed | tf_op | source)
XLA Modules:
  0.0 114.6 jit_solution(10211920169521318540)
XLA Ops:
  0.6 110.9 %column_attention_grad.1 = (bf16[3,8,64,512]{3,2,1,0:T(8,128)(2,1)}, bf16[2,3,256,512]{3,2,1,0:T(8,128)(2,1)}) custom-call(s32[2,256]{1,0:T(2,128)} %bitcast.7, s32[8]{0:T(128)} %cnt_in.1, bf16[512,1024]{1,0:T(8,128)(2,1)} %og_in.1, bf16[512,8192]{1,0:T(8,128)(2,1)} %w_in.1, bf16[8,64,512]{2,1,0:T(8,128)(2,1)} %bitcast.4, bf16[256,512]{1,0:T(8,128)(2,1)} %bitcast.5, ...), custom_call_target="tpu_custom_call" | custom-call | tf_op jit(solution)/shard_map/column_attention_grad/pallas_call | solution.py:578
  111.6 3.0 %sums_of_sides.1 = (bf16[512,512]{1,0:T(8,128)(2,1)}, bf16[2,128,512]{2,1,0:T(8,128)(2,1)}, bf16[2,128,512]{2,1,0:T(8,128)(2,1)}) custom-call(bf16[3,8,64,512]{3,2,1,0:T(8,128)(2,1)} %get-tuple-element.5.dq_in, bf16[2,3,256,512]{3,2,1,0:T(8,128)(2,1)} %get-tuple-element.6.dkv_in), custom_call_target="tpu_custom_call" | custom-call | tf_op jit(solution)/shard_map/sums_of_sides/pallas_call | solution.py:600

commit v3 on v2

--- a/solution.py
+++ b/solution.py
@@ -30,7 +30,9 @@
         return self.at.setdefault(name, len(self.at))
 
 
-MAX_COPIES = 120
+MAX_COPIES = 144
+GROUPS = ((0, 0, 2), (1, 2, 2), (2, 4, 2), (3, 6, 1), (4, 7, 1))
+HALVES = ((0, 0, 4), (1, 4, 4))
 LOCAL_IN = 12
 BLK, OTHER, PAIR, MINE, EXISTS, PLACE, PARITY = 0, 32, 64, 128, 192, 224, 256
 
@@ -76,7 +78,6 @@
     seq, mp = lax.axis_index("seq"), lax.axis_index("mp")
     y, z = seq // NZ, seq % NZ
     x, core = mp // 2, mp % 2
-    part = BLOCK * 2
 
     def at_x(d):
         return (seq, ((x + d) % NX) * 2 + core)
@@ -165,8 +166,8 @@
             send(("kvR", 1, a, e), src, kv_piece(a, z, e), at_z(1))
             send(("kvL", 1, a, e), src, kv_piece(a, z, e), at_z(-1))
 
-    def kv_hop(k):
-        for a, e in pieces:
+    def kv_hop(k, a):
+        for e in range(2):
             if k < 4 or e == 0:
                 o = zz(-k)
                 recv(("kvR", k, a, e), kv_piece(a, o, e))
@@ -178,22 +179,22 @@
                 if k < 3 or (k == 3 and e == 1):
                     send(("kvL", k + 1, a, e), kv_piece(a, o, e), kv_piece(a, o, e), at_z(-1))
 
-    def y_rows(d, h, n=4):
-        return pl.ds(((y + d) % NY) * 8 + h * n, n)
-
-    def y_first(tag, src, buf, h, n, way):
-        send((tag, way, h), src, buf.at[y_rows(0, h, n)], at_y(1 if way == "R" else -1))
-
-    def y_on(tag, buf, h, n):
-        even = h % 2 == 0
-        rows = buf.at[y_rows(-1 if even else 1, h, n)]
-        recv((tag, "R" if even else "L", h), rows)
-        send((tag, "F", h), rows, rows, at_y(1 if even else -1))
-
-    def y_rest(tag, buf, h, n):
-        even = h % 2 == 0
-        recv((tag, "L" if even else "R", h), buf.at[y_rows(1 if even else -1, h, n)])
-        recv((tag, "F", h), buf.at[y_rows(2, h, n)])
+    def y_rows(d, part):
+        return pl.ds(((y + d) % NY) * 8 + part[1], part[2])
+
+    def y_first(tag, src, buf, part, way):
+        send((tag, way, part[0]), src, buf.at[y_rows(0, part)], at_y(1 if way == "R" else -1))
+
+    def y_on(tag, buf, part):
+        even = part[0] % 2 == 0
+        rows = buf.at[y_rows(-1 if even else 1, part)]
+        recv((tag, "R" if even else "L", part[0]), rows)
+        send((tag, "F", part[0]), rows, rows, at_y(1 if even else -1))
+
+    def y_rest(tag, buf, part):
+        even = part[0] % 2 == 0
+        recv((tag, "L" if even else "R", part[0]), buf.at[y_rows(1 if even else -1, part)])
+        recv((tag, "F", part[0]), buf.at[y_rows(2, part)])
 
     def y_direct(tag, src, buf, rows):
         mine = buf.at[pl.ds(y * rows, rows)]
@@ -204,41 +205,71 @@
         for d in (1, -1, 2):
             recv((tag, d), buf.at[pl.ds(((y - d) % NY) * rows, rows)])
 
-    def og_piece(d, t, other=False):
+    def og_piece(d, g, i=None, other=False):
         c = ((x + d) % NX) * 2 + ((1 - core) if other else core)
-        return og.at[c, pl.ds(t * part, part)]
-
-    def x_own(t, way):
-        src = og_in.at[pl.ds(t * part, part)]
-        send(("og", way, t), src, og_piece(0, t), at_x(1 if way == "R" else -1))
-
-    def x_pass(d, t):
-        piece = og_piece(d, t)
-        recv(("og", {-1: "R", 1: "L", 2: "F"}[d], t), piece)
-        if d == (-1 if t % 2 == 0 else 1):
-            send(("og", "F", t), piece, piece, at_x(-d))
-        send(("ogc", d, t), piece, piece, sibling)
-
-    def mm(d, t, n=1):
-        rows = pl.ds(t * part, n * part)
+        return og.at[c, og_rows(g, i)]
+
+    def og_rows(g, i=None):
+        _, b0, n = GROUPS[g]
+        if i is None:
+            return pl.ds(b0 * BLOCK, n * BLOCK)
+        return pl.ds(b0 * BLOCK + i * (n * BLOCK // 2), n * BLOCK // 2)
+
+    def x_own(way, g, i):
+        if g < len(GROUPS):
+            send(("og", way, g, i), og_in.at[og_rows(g, i)], og_piece(0, g, i), at_x(1 if way == "R" else -1))
+
+    def x_start():
+        for n in range(3):
+            x_own("R", n // 2, n % 2)
+            x_own("L", n // 2, 1 - n % 2)
+
+    def x_on(g):
+        for way, i, d in (("R", 0, -1), ("L", 1, 1)):
+            piece = og_piece(d, g, i)
+            recv(("og", way, g, i), piece)
+            send(("og", "F", g, i), piece, piece, at_x(-d))
+            x_own(way, g + 1, 1 - i)
+            x_own(way, g + 2, i)
+
+    def x_near(g):
+        for way, i, d in (("R", 1, -1), ("L", 0, 1)):
+            recv(("og", way, g, i), og_piece(d, g, i))
+            piece = og_piece(d, g)
+            send(("ogc", d, g), piece, piece, sibling)
+
+    def x_far(g):
+        for i in range(2):
+            recv(("og", "F", g, i), og_piece(2, g, i))
+        piece = og_piece(2, g)
+        send(("ogc", 2, g), piece, piece, sibling)
+
+    def mm_own():
+        for c in (mp, x * 2 + 1 - core):
+            p = lax.dot_general(og[c], w[c], NT, preferred_element_type=F32)
+            if c is mp:
+                acc[...] = p
+                recv(("ogc", 0), og.at[x * 2 + 1 - core])
+            else:
+                acc[...] += p
+
+    def mm(d, g):
+        rows = og_rows(g)
         for other in (False, True):
             c = ((x + d) % NX) * 2 + ((1 - core) if other else core)
-            if other and d == 0:
-                recv(("ogc", 0), og.at[c])
-            elif other:
-                for i in range(t, t + n):
-                    recv(("ogc", d, i), og_piece(d, i, True))
-            p = lax.dot_general(og[c, rows, :], w[c], NT, preferred_element_type=F32)
-            if d == 0 and not other:
-                acc[rows, :] = p
-            else:
-                acc[rows, :] += p
-
-    def grad_done(t):
-        do_all[y_rows(0, t, 2)] = acc[pl.ds(t * part, part), :].astype(BF16).reshape(2, BLOCK, heads * HEAD)
-        src = do_all.at[y_rows(0, t, 2)]
+            if other:
+                recv(("ogc", d, g), og_piece(d, g, None, True))
+            acc[rows, :] += lax.dot_general(og[c, rows, :], w[c], NT, preferred_element_type=F32)
+
+    def grad_done(g):
+        n = GROUPS[g][2]
+        do_all[y_rows(0, GROUPS[g])] = acc[og_rows(g), :].astype(BF16).reshape(n, BLOCK, heads * HEAD)
+        src = do_all.at[y_rows(0, GROUPS[g])]
         for way in ("R", "L"):
-            y_first("do", src, do_all, t, 2, way)
+            y_first("do", src, do_all, GROUPS[g], way)
+
+    def do_on(g):
+        y_on("do", do_all, GROUPS[g])
 
     lane_reader = lax.broadcasted_iota(jnp.int32, (8, RDR * BLOCK), 1) // BLOCK
 
@@ -372,107 +403,119 @@
         rows = pl.ds(e * 128, 128)
         dkv[a, o, rows, :] = (dkv[a, o, rows, :].astype(F32) + buf[a, k, rows, :].astype(F32)).astype(BF16)
 
-    def rs_round(a, k):
-        for e in range(2):
-            for way, far in (("R", 0), ("L", 1)):
-                if k > 0 or e == far:
-                    rs_hop(way, a, k, e)
-
+    def rs_far(a, k):
+        rs_hop("R", a, k, 0)
+        rs_hop("L", a, k, 1)
+
+    def rs_near(a, k):
+        rs_hop("R", a, k, 1)
+        rs_hop("L", a, k, 0)
+
+    x_start()
     kv_first()
-    for t in range(3):
-        x_own(t, "R")
-        x_own(t, "L")
     for h in range(2):
-        src = q_in.at[pl.ds(h * 4, 4)], q_in.at[pl.ds(4 - h * 4, 4)]
-        y_first("q", src[0], q_all, h, 4, "R")
-        y_first("q", src[1], q_all, 1 - h, 4, "L")
+        for way, part in (("R", HALVES[h]), ("L", HALVES[1 - h])):
+            y_first("q", q_in.at[pl.ds(part[1], part[2])], q_all, part, way)
     send(("ogc", 0), og_in, og.at[mp], sibling)
     y_direct("cnt", None, cnt_all, 8)
     lax.fori_loop(0, RDR, tables, 0)
 
-    for h in range(2):
-        y_on("q", q_all, h, 4)
-    x_pass(-1, 0)
-    x_pass(1, 0)
-    x_own(3, "L")
-    kv_hop(1)
-    x_pass(-1, 1)
-    x_pass(1, 1)
+    x_on(0)
+    for part in HALVES:
+        y_on("q", q_all, part)
+    kv_hop(1, 0)
+    x_near(0)
     for cp in local:
         cp.wait()
-    mm(0, 0, 4)
-    for h in range(2):
-        y_rest("q", q_all, h, 4)
+    x_on(1)
+    mm_own()
+    kv_hop(1, 1)
+    x_far(0)
+    for d in (-1, 1, 2):
+        mm(d, 0)
+    grad_done(0)
+    x_near(1)
+    for part in HALVES:
+        y_rest("q", q_all, part)
     y_direct_wait("cnt", cnt_all, 8)
+    x_on(2)
+    kv_hop(2, 0)
     scores(0)
-    x_pass(-1, 2)
-    x_own(3, "R")
-    x_pass(1, 2)
+    for d in (-1, 1):
+        mm(d, 1)
+    x_far(1)
+    mm(2, 1)
+    grad_done(1)
+    do_on(0)
+    x_near(2)
+    kv_hop(2, 1)
+    x_on(3)
+    for d in (-1, 1):
+        mm(d, 2)
     scores(1)
-    mm(-1, 0, 3)
-    mm(1, 0, 3)
-
-    kv_hop(2)
-    x_pass(2, 0)
-    x_pass(1, 3)
-    mm(2, 0)
-    grad_done(0)
-    mm(1, 3)
-    scores(2)
-
-    x_pass(2, 1)
-    x_pass(2, 2)
-    mm(2, 1, 2)
-    grad_done(1)
+    x_far(2)
+    mm(2, 2)
     grad_done(2)
-    y_on("do", do_all, 0, 2)
-    kv_hop(3)
-    x_pass(-1, 3)
-    x_pass(2, 3)
-    mm(-1, 3)
+    do_on(1)
+    kv_hop(3, 0)
+    x_near(3)
+    x_on(4)
+    for d in (-1, 1):
+        mm(d, 3)
+    x_far(3)
     mm(2, 3)
     grad_done(3)
-    for t in (1, 2):
-        y_on("do", do_all, t, 2)
+    x_near(4)
+    do_on(2)
+    for d in (-1, 1):
+        mm(d, 4)
+    x_far(4)
+    kv_hop(3, 1)
+    mm(2, 4)
+    grad_done(4)
+    scores(2)
+    do_on(3)
     scores(3)
-    kv_hop(4)
-    y_on("do", do_all, 3, 2)
+    kv_hop(4, 0)
     scores(4)
     y_direct("st1", None, st1, OWN)
-    for t in range(3):
-        y_rest("do", do_all, t, 2)
+    do_on(4)
+    kv_hop(4, 1)
+    for g in range(4):
+        y_rest("do", do_all, GROUPS[g])
     y_direct_wait("st1", st1, OWN)
     factors()
-    y_rest("do", do_all, 3, 2)
+    y_rest("do", do_all, GROUPS[4])
 
     per_owner(value_one, 4)
-    rs_round(1, 0)
+    rs_far(1, 0)
     per_owner(value_one, 3)
-    rs_hop("R", 1, 1, 1)
-    rs_hop("L", 1, 1, 0)
-    for d in (2, 1, 0):
+    rs_near(1, 1)
+    per_owner(value_one, 2)
+    per_owner(dots_one, 4)
+    rs_far(1, 1)
+    for d in (1, 0):
         per_owner(value_one, d)
-    for d in (4, 3):
+    rs_near(1, 2)
+    for d in (3, 2):
         per_owner(dots_one, d)
-    rs_hop("R", 1, 1, 0)
-    rs_hop("L", 1, 1, 1)
-    for d in (2, 1, 0):
+    rs_far(1, 2)
+    for d in (1, 0):
         per_owner(dots_one, d)
     y_direct("st2", None, st2, OWN)
-    rs_round(1, 2)
+    rs_near(1, 3)
     y_direct_wait("st2", st2, OWN)
 
     per_owner(key_one, 4)
-    rs_round(0, 0)
+    rs_far(0, 0)
     per_owner(key_one, 3)
-    rs_hop("R", 0, 1, 1)
-    rs_hop("L", 0, 1, 0)
+    rs_near(0, 1)
+    rs_far(1, 3)
     per_owner(key_one, 2)
-    rs_round(1, 3)
-    rs_hop("R", 0, 1, 0)
-    rs_hop("L", 0, 1, 1)
-    for d in (1, 0):
-        per_owner(key_one, d)
+    rs_far(0, 1)
+    per_owner(key_one, 1)
+    rs_near(0, 2)
+    per_owner(key_one, 0)
     for a in range(2):
         local_copy(dkv.at[a, z], dkv_out.at[a, 0])
 
@@ -489,7 +532,7 @@
     lax.fori_loop(0, RDR, blocks, 0)
 
     def dq_rows(d, h):
-        return dqb.at[y_rows(d, h)]
+        return dqb.at[y_rows(d, HALVES[h])]
 
     def dq_land(way, h):
         return dq_out.at[1 if way == "R" else 2, pl.ds(h * 4, 4)]
@@ -500,24 +543,24 @@
     send(("dq", "L", 0), dq_rows(-1, 0), dq_land("L", 0), at_y(-1))
     local_copy(dqb.at[pl.ds(y * 8, 8)], dq_out.at[0])
 
-    rs_round(0, 2)
-
     def dq_on(way, h, d):
         far = pl.ds(h * 4, 4)
         recv(("dq", way, "far"), dq_far.at[far])
-        rows = y_rows(d, h)
+        rows = y_rows(d, HALVES[h])
         dqb[rows] = (dqb[rows].astype(F32) + dq_far[far].astype(F32)).astype(BF16)
         send(("dq", way, h), dqb.at[rows], dq_land(way, h), at_y(d))
 
+    rs_far(0, 2)
+    rs_near(0, 3)
     dq_on("R", 0, 1)
     dq_on("L", 1, -1)
+    rs_far(0, 3)
 
     def rs_last(a):
         for e in range(2):
             for way in ("R", "L"):
                 recv(("rs" + way, a, 3, e), rs_buf(way, a, 3, e))
 
-    rs_round(0, 3)
     for cp in local[LOCAL_IN:]:
         cp.wait()
     rs_last(1)

time: 115 us -> 110 us (0.957)
  Pallas kernels: 114 us -> 109 us
    pallas_call x1, Pallas kernels: 111 us -> 106 us  [on_device(): pl.pallas_call(functools.partial(body, heads), out_shape=(jax.ShapeDtypeS...]
where the time goes in v3:
time: 110 us
  Pallas kernels  109 us (99%)
    pallas_call x1, Pallas kernels, on_device(): pl.pallas_call(functools.partial(body, heads), out_shape=(jax.ShapeDtypeS...  106 us
    pallas_call x1, Pallas kernels, on_device(): pl.pallas_call(sums, out_shape=(jax.ShapeDtypeStruct(queries.shape, BF16)...  3.04 us

profile of v3, /device:TPU:8, one launch (start us, length us, event | category | flops | bytes accessed | tf_op | source)
XLA Modules:
  0.0 109.5 jit_solution(199366995673113165)
XLA Ops:
  0.6 105.8 %column_attention_grad.1 = (bf16[3,8,64,512]{3,2,1,0:T(8,128)(2,1)}, bf16[2,3,256,512]{3,2,1,0:T(8,128)(2,1)}) custom-call(s32[2,256]{1,0:T(2,128)} %bitcast.7, s32[8]{0:T(128)} %cnt_in.1, bf16[512,1024]{1,0:T(8,128)(2,1)} %og_in.1, bf16[512,8192]{1,0:T(8,128)(2,1)} %w_in.1, bf16[8,64,512]{2,1,0:T(8,128)(2,1)} %bitcast.4, bf16[256,512]{1,0:T(8,128)(2,1)} %bitcast.5, ...), custom_call_target="tpu_custom_call" | custom-call | tf_op jit(solution)/shard_map/column_attention_grad/pallas_call | solution.py:621
  106.5 3.0 %sums_of_sides.1 = (bf16[512,512]{1,0:T(8,128)(2,1)}, bf16[2,128,512]{2,1,0:T(8,128)(2,1)}, bf16[2,128,512]{2,1,0:T(8,128)(2,1)}) custom-call(bf16[3,8,64,512]{3,2,1,0:T(8,128)(2,1)} %get-tuple-element.5.dq_in, bf16[2,3,256,512]{3,2,1,0:T(8,128)(2,1)} %get-tuple-element.6.dkv_in), custom_call_target="tpu_custom_call" | custom-call | tf_op jit(solution)/shard_map/sums_of_sides/pallas_call | solution.py:643

commit v4 on v3

--- a/solution.py
+++ b/solution.py
@@ -47,7 +47,8 @@
     k_in,
     v_in,
     dq_out,
-    dkv_out,
+    dk_out,
+    dv_out,
     og,
     w,
     acc,
@@ -68,6 +69,8 @@
     rsl,
     dqb,
     dq_far,
+    dq_r,
+    dq_l,
     scal,
     ssem,
     rsem,
@@ -94,6 +97,12 @@
         return (z + d) % NZ
 
     started = []
+    drained = [0]
+
+    def drain(leave=0):
+        for cp in started[drained[0] : len(started) - leave]:
+            cp.wait_send()
+        drained[0] = max(drained[0], len(started) - leave)
 
     def send(name, src, dst, dev):
         i = ids(*name)
@@ -384,8 +393,8 @@
 
     def rs_buf(way, a, k, e):
         rows = pl.ds(e * 128, 128)
-        if k == 3:
-            return dkv_out.at[a, 1 if way == "R" else 2, rows]
+        if k == 3 and a == 0:
+            return dk_out.at[1 if way == "R" else 2, rows]
         return (rsr if way == "R" else rsl).at[a, k, rows]
 
     def rs_hop(way, a, k, e):
@@ -503,21 +512,21 @@
     for d in (1, 0):
         per_owner(dots_one, d)
     y_direct("st2", None, st2, OWN)
-    rs_near(1, 3)
+    drain(14)
     y_direct_wait("st2", st2, OWN)
 
     per_owner(key_one, 4)
     rs_far(0, 0)
     per_owner(key_one, 3)
     rs_near(0, 1)
-    rs_far(1, 3)
+    rs_near(1, 3)
     per_owner(key_one, 2)
     rs_far(0, 1)
     per_owner(key_one, 1)
     rs_near(0, 2)
+    rs_far(1, 3)
     per_owner(key_one, 0)
-    for a in range(2):
-        local_copy(dkv.at[a, z], dkv_out.at[a, 0])
+    local_copy(dkv.at[0, z], dk_out.at[0])
 
     def blocks(r, carry):
         def one(b, carry2):
@@ -535,13 +544,12 @@
         return dqb.at[y_rows(d, HALVES[h])]
 
     def dq_land(way, h):
-        return dq_out.at[1 if way == "R" else 2, pl.ds(h * 4, 4)]
+        return (dq_r if way == "R" else dq_l).at[pl.ds(h * 4, 4)]
 
     send(("dq", "R", "far"), dq_rows(2, 0), dq_far.at[pl.ds(0, 4)], at_y(1))
     send(("dq", "L", "far"), dq_rows(2, 1), dq_far.at[pl.ds(4, 4)], at_y(-1))
     send(("dq", "R", 1), dq_rows(1, 1), dq_land("R", 1), at_y(1))
     send(("dq", "L", 0), dq_rows(-1, 0), dq_land("L", 0), at_y(-1))
-    local_copy(dqb.at[pl.ds(y * 8, 8)], dq_out.at[0])
 
     def dq_on(way, h, d):
         far = pl.ds(h * 4, 4)
@@ -561,26 +569,44 @@
             for way in ("R", "L"):
                 recv(("rs" + way, a, 3, e), rs_buf(way, a, 3, e))
 
-    for cp in local[LOCAL_IN:]:
-        cp.wait()
+    def three(a, b, c):
+        return (a.astype(F32) + b.astype(F32) + c.astype(F32)).astype(BF16)
+
     rs_last(1)
+    dkv[1, z] = three(dkv[1, z], rsr[1, 3], rsl[1, 3])
+    local_copy(dkv.at[1, z], dv_out)
     for h in range(2):
         for way in ("R", "L"):
             recv(("dq", way, h), dq_land(way, h))
+    own = pl.ds(y * 8, 8)
+    dqb[own] = three(dqb[own], dq_r[...], dq_l[...])
+    local_copy(dqb.at[own], dq_out)
+    drain(4)
+    for cp in local[LOCAL_IN:]:
+        cp.wait()
     rs_last(0)
-    for cp in started:
-        cp.wait_send()
-
-
-def sums(dq_in, dkv_in, dq_out, dk_out, dv_out):
-    def three(t):
-        return (t[0].astype(F32) + t[1].astype(F32) + t[2].astype(F32)).astype(BF16)
-
-    for b in range(8):
-        dq_out[pl.ds(b * BLOCK, BLOCK), :] = three(dq_in[:, b])
-    for out, a in ((dk_out, 0), (dv_out, 1)):
-        for e in range(2):
-            out[e] = three(dkv_in[a, :, pl.ds(e * 128, 128), :])
+    drain()
+
+
+def finish(dq_in, dk_in, dv_in, dq_out, dk_out, dv_out, dq, dk, dv, total, sem):
+    takes = [
+        pltpu.make_async_copy(src, dst, sem.at[i])
+        for i, (src, dst) in enumerate(((dk_in, dk), (dv_in, dv), (dq_in, dq)))
+    ]
+    gives = [
+        pltpu.make_async_copy(src, dst, sem.at[3 + i])
+        for i, (src, dst) in enumerate(((total, dk_out), (dv, dv_out), (dq, dq_out)))
+    ]
+    for take in takes:
+        take.start()
+    takes[0].wait()
+    total[...] = (dk[0].astype(F32) + dk[1].astype(F32) + dk[2].astype(F32)).astype(BF16)
+    gives[0].start()
+    for i in (1, 2):
+        takes[i].wait()
+        gives[i].start()
+    for give in gives:
+        give.wait()
 
 
 def on_device(out_grad, out_weight, queries, keys, values, retrieval, counts):
@@ -606,9 +632,11 @@
         vm((OWN, 8, lanes), F32),
         vm((OWN * RDR, BLOCK, width), BF16),
         vm((2, OWN, 256, width), BF16),
-        vm((2, 3, 256, width), BF16),
-        vm((2, 3, 256, width), BF16),
+        vm((2, 4, 256, width), BF16),
+        vm((2, 4, 256, width), BF16),
         vm((RDR * blocks, BLOCK, width), BF16),
+        vm((8, BLOCK, width), BF16),
+        vm((8, BLOCK, width), BF16),
         vm((8, BLOCK, width), BF16),
         pltpu.SMEM((288,), jnp.int32),
         pltpu.SemaphoreType.DMA((MAX_COPIES,)),
@@ -616,16 +644,16 @@
         pltpu.SemaphoreType.DMA((16,)),
     ]
     hbm = pl.BlockSpec(memory_space=pl.ANY)
-    vmem = pl.BlockSpec(memory_space=pltpu.VMEM)
     smem = pl.BlockSpec(memory_space=pltpu.SMEM)
-    dq_parts, dkv_parts = pl.pallas_call(
+    dq, dk_parts, dv = pl.pallas_call(
         functools.partial(body, heads),
         out_shape=(
-            jax.ShapeDtypeStruct((3, blocks, BLOCK, width), BF16),
-            jax.ShapeDtypeStruct((2, 3, 256, width), BF16),
+            jax.ShapeDtypeStruct((blocks, BLOCK, width), BF16),
+            jax.ShapeDtypeStruct((3, 256, width), BF16),
+            jax.ShapeDtypeStruct((256, width), BF16),
         ),
         in_specs=[smem, smem, hbm, hbm, hbm, hbm, hbm],
-        out_specs=(hbm, hbm),
+        out_specs=(hbm, hbm, hbm),
         scratch_shapes=scratch,
         compiler_params=pltpu.CompilerParams(
             collective_id=0, has_side_effects=True, vmem_limit_bytes=63 * 1024 * 1024
@@ -640,17 +668,25 @@
         keys.reshape(256, width),
         values.reshape(256, width),
     )
-    return pl.pallas_call(
-        sums,
+    dq, dk, dv = pl.pallas_call(
+        finish,
         out_shape=(
-            jax.ShapeDtypeStruct(queries.shape, BF16),
-            jax.ShapeDtypeStruct(keys.shape, BF16),
-            jax.ShapeDtypeStruct(values.shape, BF16),
+            jax.ShapeDtypeStruct((blocks, BLOCK, width), BF16),
+            jax.ShapeDtypeStruct((256, width), BF16),
+            jax.ShapeDtypeStruct((256, width), BF16),
         ),
-        in_specs=[vmem, vmem],
-        out_specs=(vmem, vmem, vmem),
-        name="sums_of_sides",
-    )(dq_parts, dkv_parts)
+        in_specs=[hbm, hbm, hbm],
+        out_specs=(hbm, hbm, hbm),
+        scratch_shapes=[
+            vm((blocks, BLOCK, width), BF16),
+            vm((3, 256, width), BF16),
+            vm((256, width), BF16),
+            vm((256, width), BF16),
+            pltpu.SemaphoreType.DMA((6,)),
+        ],
+        name="finish_outputs",
+    )(dq, dk_parts, dv)
+    return dq.reshape(queries.shape), dk.reshape(keys.shape), dv.reshape(values.shape)
 
 
 def solution(mesh):

time: 110 us -> 108 us (0.982)
  Pallas kernels: 109 us -> 106 us
    pallas_call x1, Pallas kernels: 106 us -> 104 us  [on_device(): pl.pallas_call(functools.partial(body, heads), out_shape=(jax.ShapeDtypeS...]
where the time goes in v4:
time: 108 us; the launch traced here: 107 us
  Pallas kernels  106 us (98%)
    pallas_call x1, Pallas kernels, on_device(): pl.pallas_call(functools.partial(body, heads), out_shape=(jax.ShapeDtypeS...  104 us
    pallas_call x1, Pallas kernels, on_device(): pl.pallas_call(finish, out_shape=(jax.ShapeDtypeStruct((blocks, BLOCK, wi...  2.25 us

profile of v4, /device:TPU:8, one launch (start us, length us, event | category | flops | bytes accessed | tf_op | source)
XLA Modules:
  0.0 107.1 jit_solution(3737020312285183000)
XLA Ops:
  0.6 104.0 %column_attention_grad.1 = (bf16[8,64,512]{2,1,0:T(8,128)(2,1)}, bf16[3,256,512]{2,1,0:T(8,128)(2,1)}, bf16[256,512]{1,0:T(8,128)(2,1)}) custom-call(s32[2,256]{1,0:T(2,128)} %bitcast.10, s32[8]{0:T(128)} %cnt_in.1, bf16[512,1024]{1,0:T(8,128)(2,1)} %og_in.1, bf16[512,8192]{1,0:T(8,128)(2,1)} %w_in.1, bf16[8,64,512]{2,1,0:T(8,128)(2,1)} %bitcast.7, ...), custom_call_target="tpu_custom_call" | custom-call | tf_op jit(solution)/shard_map/column_attention_grad/pallas_call | solution.py:648
  104.7 2.2 %finish_outputs.1 = (bf16[8,64,512]{2,1,0:T(8,128)(2,1)}, bf16[256,512]{1,0:T(8,128)(2,1)}, bf16[256,512]{1,0:T(8,128)(2,1)}) custom-call(bf16[8,64,512]{2,1,0:T(8,128)(2,1)} %get-tuple-element.9.dq_in, bf16[3,256,512]{2,1,0:T(8,128)(2,1)} %get-tuple-element.10.dk_in, bf16[256,512]{1,0:T(8,128)(2,1)} %get-tuple-element.11.dv_in), custom_call_target="tpu_custom_call" | custom-call | tf_op jit(solution)/shard_map/finish_outputs/pallas_call | solution.py:671

commit v5 on v4

--- a/solution.py
+++ b/solution.py
@@ -33,14 +33,14 @@
 MAX_COPIES = 144
 GROUPS = ((0, 0, 2), (1, 2, 2), (2, 4, 2), (3, 6, 1), (4, 7, 1))
 HALVES = ((0, 0, 4), (1, 4, 4))
-LOCAL_IN = 12
+LOCAL_IN = 14
 BLK, OTHER, PAIR, MINE, EXISTS, PLACE, PARITY = 0, 32, 64, 128, 192, 224, 256
 
 
 def body(
     heads,
-    ret,
-    cnt_in,
+    ret_in,
+    cnt_hbm,
     og_in,
     w_in,
     q_in,
@@ -71,6 +71,8 @@
     dq_far,
     dq_r,
     dq_l,
+    ret,
+    cnt_in,
     scal,
     ssem,
     rsem,
@@ -130,6 +132,8 @@
         cp.start()
         local.append(cp)
 
+    local_copy(ret_in, ret)
+    local_copy(cnt_hbm, cnt_in)
     local_copy(og_in, og.at[mp])
     for c in range(2 * NX):
         local_copy(w_in.at[:, pl.ds(c * 1024, 1024)], w.at[c])
@@ -159,8 +163,10 @@
             scal[EXISTS + o * RDR + r] = t >> 10
         return carry
 
-    for b in range(8):
-        cnt_all[y * 8 + b] = jnp.full((8, RDR * BLOCK), cnt_in[b].astype(F32))
+    def count_rows():
+        for b in range(8):
+            cnt_all[y * 8 + b] = jnp.full((8, RDR * BLOCK), cnt_in[b].astype(F32))
+
 
     pl.semaphore_wait(barrier, len(peers))
 
@@ -426,6 +432,9 @@
         for way, part in (("R", HALVES[h]), ("L", HALVES[1 - h])):
             y_first("q", q_in.at[pl.ds(part[1], part[2])], q_all, part, way)
     send(("ogc", 0), og_in, og.at[mp], sibling)
+    for cp in local[:2]:
+        cp.wait()
+    count_rows()
     y_direct("cnt", None, cnt_all, 8)
     lax.fori_loop(0, RDR, tables, 0)
 
@@ -434,7 +443,7 @@
         y_on("q", q_all, part)
     kv_hop(1, 0)
     x_near(0)
-    for cp in local:
+    for cp in local[2:]:
         cp.wait()
     x_on(1)
     mm_own()
@@ -500,18 +509,14 @@
     rs_far(1, 0)
     per_owner(value_one, 3)
     rs_near(1, 1)
-    per_owner(value_one, 2)
-    per_owner(dots_one, 4)
-    rs_far(1, 1)
-    for d in (1, 0):
+    for d in (2, 1, 0):
         per_owner(value_one, d)
-    rs_near(1, 2)
-    for d in (3, 2):
-        per_owner(dots_one, d)
-    rs_far(1, 2)
-    for d in (1, 0):
+    for d in (4, 3, 2, 1, 0):
         per_owner(dots_one, d)
     y_direct("st2", None, st2, OWN)
+    rs_far(1, 1)
+    rs_near(1, 2)
+    rs_far(1, 2)
     drain(14)
     y_direct_wait("st2", st2, OWN)
 
@@ -638,13 +643,14 @@
         vm((8, BLOCK, width), BF16),
         vm((8, BLOCK, width), BF16),
         vm((8, BLOCK, width), BF16),
+        pltpu.SMEM((2, 256), jnp.int32),
+        pltpu.SMEM((8,), jnp.int32),
         pltpu.SMEM((288,), jnp.int32),
         pltpu.SemaphoreType.DMA((MAX_COPIES,)),
         pltpu.SemaphoreType.DMA((MAX_COPIES,)),
-        pltpu.SemaphoreType.DMA((16,)),
+        pltpu.SemaphoreType.DMA((20,)),
     ]
     hbm = pl.BlockSpec(memory_space=pl.ANY)
-    smem = pl.BlockSpec(memory_space=pltpu.SMEM)
     dq, dk_parts, dv = pl.pallas_call(
         functools.partial(body, heads),
         out_shape=(
@@ -652,7 +658,7 @@
             jax.ShapeDtypeStruct((3, 256, width), BF16),
             jax.ShapeDtypeStruct((256, width), BF16),
         ),
-        in_specs=[smem, smem, hbm, hbm, hbm, hbm, hbm],
+        in_specs=[hbm] * 7,
         out_specs=(hbm, hbm, hbm),
         scratch_shapes=scratch,
         compiler_params=pltpu.CompilerParams(

time: 108 us -> 106 us (0.981); the launches traced: 107 us -> 106 us
  no operation moved by 1% of the time
where the time goes in v5:
time: 106 us
  Pallas kernels  106 us (100%)
    pallas_call x1, Pallas kernels, on_device(): pl.pallas_call(functools.partial(body, heads), out_shape=(jax.ShapeDtypeS...  103 us
    pallas_call x1, Pallas kernels, on_device(): pl.pallas_call(finish, out_shape=(jax.ShapeDtypeStruct((blocks, BLOCK, wi...  2.25 us

profile of v5, /device:TPU:8, one launch (start us, length us, event | category | flops | bytes accessed | tf_op | source)
XLA Modules:
  0.0 106.3 jit_solution(6981245813334300572)
XLA Ops:
  0.6 103.3 %column_attention_grad.1 = (bf16[8,64,512]{2,1,0:T(8,128)(2,1)}, bf16[3,256,512]{2,1,0:T(8,128)(2,1)}, bf16[256,512]{1,0:T(8,128)(2,1)}) custom-call(s32[2,256]{1,0:T(2,128)} %bitcast.10, s32[8]{0:T(128)} %cnt_hbm.1, bf16[512,1024]{1,0:T(8,128)(2,1)} %og_in.1, bf16[512,8192]{1,0:T(8,128)(2,1)} %w_in.1, bf16[8,64,512]{2,1,0:T(8,128)(2,1)} %bitcast.7, ...), custom_call_target="tpu_custom_call" | custom-call | tf_op jit(solution)/shard_map/column_attention_grad/pallas_call | solution.py:654
  103.9 2.2 %finish_outputs.1 = (bf16[8,64,512]{2,1,0:T(8,128)(2,1)}, bf16[256,512]{1,0:T(8,128)(2,1)}, bf16[256,512]{1,0:T(8,128)(2,1)}) custom-call(bf16[8,64,512]{2,1,0:T(8,128)(2,1)} %get-tuple-element.9.dq_in, bf16[3,256,512]{2,1,0:T(8,128)(2,1)} %get-tuple-element.10.dk_in, bf16[256,512]{1,0:T(8,128)(2,1)} %get-tuple-element.11.dv_in), custom_call_target="tpu_custom_call" | custom-call | tf_op jit(solution)/shard_map/finish_outputs/pallas_call | solution.py:677

commit v6 on v5

--- a/solution.py
+++ b/solution.py
@@ -60,6 +60,7 @@
     do_own,
     ex,
     gw,
+    low,
     st1,
     st2,
     fac,
@@ -356,13 +357,25 @@
     def both(o, h, t0, t1):
         return jnp.concatenate([t0.astype(BF16), t1.astype(BF16)], axis=0)
 
-    def value_one(o):
+    def weights(o, h):
+        e = ex[o, h]
+        return both(o, h, e * fac[o, h : h + 1, :], e * fac[o, heads + h : heads + h + 1, :])
+
+    def weights_one(o):
+        for h in range(heads):
+            low[o, h] = weights(o, h)
+
+    def value_with(o, of):
         gather_blocks(do_all, do_own, o)
         for h in range(heads):
-            e = ex[o, h]
-            p = both(o, h, e * fac[o, h : h + 1, :], e * fac[o, heads + h : heads + h + 1, :])
-            t = lax.dot_general(p, do_own[o, :, cols(h)], NN, preferred_element_type=F32)
+            t = lax.dot_general(of(o, h), do_own[o, :, cols(h)], NN, preferred_element_type=F32)
             dkv[1, o, :, cols(h)] = t.astype(BF16)
+
+    def value_one(o):
+        value_with(o, weights)
+
+    def value_first(o):
+        value_with(o, lambda o, h: low[o, h])
 
     def dots_one(o):
         par = lane_pick(PARITY, o)
@@ -503,11 +516,13 @@
         y_rest("do", do_all, GROUPS[g])
     y_direct_wait("st1", st1, OWN)
     factors()
+    for d in (4, 3):
+        per_owner(weights_one, d)
     y_rest("do", do_all, GROUPS[4])
 
-    per_owner(value_one, 4)
+    per_owner(value_first, 4)
     rs_far(1, 0)
-    per_owner(value_one, 3)
+    per_owner(value_first, 3)
     rs_near(1, 1)
     for d in (2, 1, 0):
         per_owner(value_one, d)
@@ -632,6 +647,7 @@
         vm((OWN, lanes, width), BF16),
         vm((OWN, heads, 128, lanes), F32),
         vm((OWN, heads, 128, lanes), F32),
+        vm((OWN, heads, 256, lanes), BF16),
         vm((NY * OWN, 8, lanes), F32),
         vm((NY * OWN, 8, lanes), F32),
         vm((OWN, 8, lanes), F32),

time: 106 us -> 106 us (level)
  no operation moved by 1% of the time
where the time goes in v6:
time: 106 us
  Pallas kernels  106 us (100%)
    pallas_call x1, Pallas kernels, on_device(): pl.pallas_call(functools.partial(body, heads), out_shape=(jax.ShapeDtypeS...  103 us
    pallas_call x1, Pallas kernels, on_device(): pl.pallas_call(finish, out_shape=(jax.ShapeDtypeStruct((blocks, BLOCK, wi...  2.25 us

profile of v6, /device:TPU:8, one launch (start us, length us, event | category | flops | bytes accessed | tf_op | source)
XLA Modules:
  0.0 106.3 jit_solution(16674684044789916376)
XLA Ops:
  0.6 103.3 %column_attention_grad.1 = (bf16[8,64,512]{2,1,0:T(8,128)(2,1)}, bf16[3,256,512]{2,1,0:T(8,128)(2,1)}, bf16[256,512]{1,0:T(8,128)(2,1)}) custom-call(s32[2,256]{1,0:T(2,128)} %bitcast.10, s32[8]{0:T(128)} %cnt_hbm.1, bf16[512,1024]{1,0:T(8,128)(2,1)} %og_in.1, bf16[512,8192]{1,0:T(8,128)(2,1)} %w_in.1, bf16[8,64,512]{2,1,0:T(8,128)(2,1)} %bitcast.7, ...), custom_call_target="tpu_custom_call" | custom-call | tf_op jit(solution)/shard_map/column_attention_grad/pallas_call | solution.py:670
  103.9 2.2 %finish_outputs.1 = (bf16[8,64,512]{2,1,0:T(8,128)(2,1)}, bf16[256,512]{1,0:T(8,128)(2,1)}, bf16[256,512]{1,0:T(8,128)(2,1)}) custom-call(bf16[8,64,512]{2,1,0:T(8,128)(2,1)} %get-tuple-element.9.dq_in, bf16[3,256,512]{2,1,0:T(8,128)(2,1)} %get-tuple-element.10.dk_in, bf16[256,512]{1,0:T(8,128)(2,1)} %get-tuple-element.11.dv_in), custom_call_target="tpu_custom_call" | custom-call | tf_op jit(solution)/shard_map/finish_outputs/pallas_call | solution.py:693
